TPU v7x, 32 devices: a whole 2x2x4 slice. The times are simulated.
32 devices in a mesh: graph: 8 (over z, x), dp: 4 (over y, core).
Axes of the slice: x: 2, y: 2, z: 4, core: 2. Of those that a mesh axis runs over, the one named last changes fastest.
Arguments:
- node_state: bfloat16 [4, 4096, 512], P('dp', 'graph'), may hold values from -6 to 6
- edge_state: bfloat16 [4, 16384, 512], P('dp', 'graph'), may hold values from -6 to 6
- senders: int32 [4, 16384], P('dp', 'graph'), may hold values from 0 to 575
- receivers: int32 [4, 16384], P('dp', 'graph'), may hold values from 0 to 511
- send_index: int32 [4, 8, 64], P('dp', 'graph'), may hold values from 0 to 511
- cotangent: bfloat16 [4, 4096, 512], P('dp', 'graph'), may hold values from -0.09375 to 0.09375
- w_edge: bfloat16 [1536, 512], replicated, may hold values from -0.15625 to 0.15625
- w_node: bfloat16 [1024, 512], replicated, may hold values from -0.1875 to 0.1875
- error_memory: float32 [4, 1024, 512], P('dp', 'graph'), may hold values from -6 to 6
- warm_q: float32 [512, 64], replicated, may hold values from -6 to 6
Outputs:
- new_nodes: bfloat16 [4, 4096, 512], P('dp', 'graph')
- update: float32 [1024, 512], P('graph')
- new_error: float32 [4, 1024, 512], P('dp', 'graph')
- new_q: float32 [512, 64], replicated
All inputs are finite; a program needn't handle non-finite values.
Results may differ from a plain program's by a relative error of at most 0.0066.
Values may be sent and summed in bfloat16 or wider, within the bound.
No kernel may reach another device: no remote copies, remote signals or barrier semaphores. Data moves between devices by JAX's collectives and lax.ppermute only.
A program may use at most 64 MiB of HBM per device.

v0:
```python
import jax
import jax.numpy as jnp
from jax import lax
from jax.sharding import PartitionSpec as P


def silu_slope(pre_act):
    sigmoid_v = jax.nn.sigmoid(pre_act)
    return sigmoid_v * (1.0 + pre_act * (1.0 - sigmoid_v))


def body(
    node_state,
    edge_state,
    senders,
    receivers,
    send_index,
    cotangent,
    w_edge,
    w_node,
    error_memory,
    warm_q,
):
    highest = lax.Precision.HIGHEST
    node_block = node_state[0]
    edge_block = edge_state[0]
    features = node_block.shape[1]
    node_count = node_block.shape[0]
    partitions = lax.axis_size("graph")
    outgoing = node_block[send_index[0, 0]].reshape(partitions, -1, features)
    incoming = lax.all_to_all(outgoing, "graph", split_axis=0, concat_axis=0, tiled=True)
    lookup = jnp.concatenate([node_block, incoming.reshape(-1, features)], axis=0)
    sender_rows = lookup[senders[0]]
    receiver_rows = node_block[receivers[0]]
    edge_pre = jnp.dot(edge_block, w_edge[:features], preferred_element_type=jnp.float32)
    edge_pre = edge_pre + jnp.dot(
        sender_rows, w_edge[features : 2 * features], preferred_element_type=jnp.float32
    )
    edge_pre = edge_pre + jnp.dot(
        receiver_rows, w_edge[2 * features :], preferred_element_type=jnp.float32
    )
    edge_new = (edge_block.astype(jnp.float32) + jax.nn.silu(edge_pre)).astype(jnp.bfloat16)
    incidence = (receivers[0][None, :] == jnp.arange(node_count, dtype=jnp.int32)[:, None]).astype(
        jnp.bfloat16
    )
    aggregate = jnp.dot(incidence, edge_new, preferred_element_type=jnp.float32).astype(
        jnp.bfloat16
    )
    node_pre = jnp.dot(node_block, w_node[:features], preferred_element_type=jnp.float32)
    node_pre = node_pre + jnp.dot(aggregate, w_node[features:], preferred_element_type=jnp.float32)
    new_block = (node_block.astype(jnp.float32) + jax.nn.silu(node_pre)).astype(jnp.bfloat16)
    node_delta = (cotangent[0].astype(jnp.float32) * silu_slope(node_pre)).astype(jnp.bfloat16)
    grad_top = jnp.einsum("nk,nj->kj", node_block, node_delta, preferred_element_type=jnp.float32)
    grad_low = jnp.einsum("nk,nj->kj", aggregate, node_delta, preferred_element_type=jnp.float32)
    gradient = jnp.concatenate([grad_top, grad_low], axis=0)
    mine = lax.psum_scatter(gradient, "graph", scatter_dimension=0, tiled=True)
    matrix = mine + error_memory[0]
    local_left = jnp.dot(matrix, warm_q, precision=highest)
    own_left = lax.psum(local_left, "dp")
    gram = lax.psum(jnp.dot(own_left.T, own_left, precision=highest), "graph")
    factor = jnp.linalg.cholesky(gram)
    ortho = lax.linalg.triangular_solve(
        factor, own_left, left_side=False, lower=True, transpose_a=True
    )
    right_part = jnp.dot(matrix.T, ortho, precision=highest)
    new_q = lax.psum(right_part, ("graph", "dp")) / lax.axis_size("dp")
    update = jnp.dot(ortho, new_q.T, precision=highest)
    new_error = matrix - update
    return (new_block[None], update, new_error[None], new_q)


def solution(mesh):
    return jax.shard_map(
        body,
        mesh=mesh,
        in_specs=(
            P("dp", "graph", None),
            P("dp", "graph", None),
            P("dp", "graph"),
            P("dp", "graph"),
            P("dp", "graph", None),
            P("dp", "graph", None),
            P(),
            P(),
            P("dp", "graph", None),
            P(),
        ),
        out_specs=(P("dp", "graph", None), P("graph", None), P("dp", "graph", None), P()),
        check_vma=False,
    )
```

profile of v0, /device:TPU:0, one launch (start us, length us, event | category | flops | bytes accessed | tf_op | source)
XLA Modules:
  0.0 321.9 jit_solution(285913944859563682)
XLA Ops:
  7.2 0.0 copy-start
  7.2 0.0 copy-start.1
  7.2 0.7 fusion.19
  7.9 2.4 gather_fusion
  10.4 7.3 %all-to-all-start = ((bf16[8,8,512]{2,1,0:T(8,128)(2,1)}), bf16[8,8,512]{2,1,0:T(8,128)(2,1)S(1)}, u32[]{:S(2)}, u32[]{:S(2)}) async-start(bf16[8,8,512]{2,1,0:T(8,128)(2,1)} %bitcast.5), calls=%async_computation | async-start | bytes 131072 | tf_op jit(solution)/shard_map/all_to_all | solution.py:31
  17.7 0.0 reduce-scatter.2.cloned.1.call-start
  17.7 0.7 compare_select_fusion.1
  18.4 0.7 compare_select_fusion
  19.1 0.0 copy-done.1
  19.1 0.0 copy-start.8
  19.2 9.2 %gather_fusion.2 = bf16[2048,512]{1,0:T(8,128)(2,1)} fusion(bf16[512,512]{1,0:T(8,128)(2,1)S(1)} %bitcast.63, s32[2048]{0:T(1024)S(1)} %broadcast_clamp_fusion), kind=kCustom, calls=%fused_computation.2 | custom fusion | bytes 4202496 | tf_op jit(solution)/shard_map/gather | solution.py:34
  28.4 1.4 fusion.12
  29.8 0.6 copy-done.2
  30.3 4.3 %fusion.1 = f32[2048,512]{1,0:T(8,128)} fusion(bf16[1,2048,512]{2,1,0:T(8,128)(2,1)S(1)} %copy-done.2, bf16[1536,512]{1,0:T(8,128)(2,1)} %param.16), kind=kOutput, calls=%fused_computation.7 | convolution fusion | flops 1073741824 | bytes 6815744 | tf_op jit(solution)/shard_map/dot_general | solution.py:35
  34.6 0.0 all-to-all-done
  34.6 7.5 %gather_fusion.1 = bf16[2048,512]{1,0:T(8,128)(2,1)S(1)} fusion(bf16[576,512]{1,0:T(8,128)(2,1)S(1)} %pad_maximum_fusion.1, s32[2048]{0:T(1024)S(1)} %broadcast_clamp_fusion.1), kind=kCustom, calls=%fused_computation.1 | custom fusion | bytes 4202496 | tf_op jit(solution)/shard_map/gather | solution.py:33
  42.2 0.0 copy-start.10
  42.2 4.3 %fusion.9 = f32[2048,512]{1,0:T(8,128)} fusion(bf16[2048,512]{1,0:T(8,128)(2,1)S(1)} %gather_fusion.1, bf16[1536,512]{1,0:T(8,128)(2,1)} %param.16), kind=kOutput, calls=%fused_computation.20 | convolution fusion | flops 1073741824 | bytes 6815744 | tf_op jit(solution)/shard_map/dot_general | solution.py:36
  46.5 8.2 %fusion.4 = bf16[512,512]{1,0:T(8,128)(2,1)S(1)} fusion(s32[2048]{0:T(1024)S(1)} %bitcast.68, f32[2048,512]{1,0:T(8,128)} %fusion.1, f32[2048,512]{1,0:T(8,128)} %fusion.9, bf16[2048,512]{1,0:T(8,128)(2,1)} %gather_fusion.2, bf16[1,2048,512]{2,1,0:T(8,128)(2,1)} %param.11, bf16[1536,512]{1,0:T(8,128)(2,1)} %param.16), kind=kOutput, calls=%fused_computation.12 | convolution fusion | flops 2158231552 | bytes 13639680 | tf_op jit(solution)/shard_map/dot_general | solution.py:46
  54.6 0.0 copy-done.5
  54.7 0.0 copy-done.9
  54.7 2.7 fusion.5
  57.4 0.5 fusion.27
  57.8 0.5 convolution_bitcast_fusion
  58.3 1.5 pad_maximum_fusion
  59.8 0.0 reduce-scatter.2.cloned.1.call-update
  59.9 0.0 all-reduce.2.cloned.1.call-start
  59.9 69.8 %reduce-scatter.2.cloned.1.call-done = f32[128,512]{1,0:T(8,128)} async-done(((f32[1024,512]{1,0:T(8,128)}), f32[128,512]{1,0:T(8,128)}) %reduce-scatter.2.cloned.1.call-update) | async-done | bytes 262160 | tf_op jit(solution)/shard_map/reduce_scatter | solution.py:56
  129.7 0.0 copy-done.3
  129.8 1.4 fusion.24
  131.2 10.3 %psum.21 = f32[128,64]{0,1:T(8,128)S(1)} all-reduce(f32[128,64]{0,1:T(8,128)S(1)} %fusion.24), channel_id=1, replica_groups=mesh['graph'=8,'dp'=4] {'dp'}, use_global_device_ids=true, to_apply=%region_1.2 | all-reduce | flops 8192 | bytes 65536 | tf_op jit(solution)/shard_map/psum | solution.py:59
  141.4 0.2 fusion.28
  141.6 34.8 %psum.22 = f32[64,64]{0,1:T(8,128)S(1)} all-reduce(f32[64,64]{0,1:T(8,128)S(1)} %fusion.28), channel_id=1, replica_groups=mesh['graph'=8,'dp'=4] {'graph'}, use_global_device_ids=true, to_apply=%region_2.3 | all-reduce | flops 4096 | bytes 32768 | tf_op jit(solution)/shard_map/psum | solution.py:60
  176.5 0.1 copy.17
  176.6 5.9 %cholesky.16 = f32[64,64]{1,0:T(8,128)S(1)} custom-call(f32[64,64]{1,0:T(8,128)S(1)} %fusion.18), custom_call_target="Cholesky" | custom-call | tf_op jit(solution)/shard_map/jit(cholesky)/cholesky | solution.py:61
  182.5 0.6 compare_reduce_fusion
  183.1 0.7 fusion.15
  183.8 4.9 %custom-call.6 = f32[1,64,64]{1,2,0:T(8,128)S(1)} custom-call(f32[1,64,64]{2,1,0:T(8,128)S(1)} %fusion.15), custom_call_target="InvertDiagBlocksLowerTriangular" | custom-call | tf_op jit(solution)/shard_map/triangular_solve | solution.py:62
  188.7 0.2 fusion.16
  188.9 1.9 fusion.23
  190.8 0.0 all-reduce.2.cloned.1.call-update
  190.8 122.1 %all-reduce.2.cloned.1.call-done = f32[512,64]{0,1:T(8,128)} async-done(((f32[512,64]{0,1:T(8,128)}), f32[512,64]{0,1:T(8,128)}) %all-reduce.2.cloned.1.call-update) | async-done | bytes 131088 | tf_op jit(solution)/shard_map/psum | solution.py:66
  312.9 0.9 broadcast_multiply_fusion
  313.8 0.0 copy-start.7
  313.8 0.4 fusion.29
  314.3 0.0 copy-start.6
  314.3 0.8 subtract_bitcast_fusion
  315.1 0.0 copy-done.7
  (16 shorter events, 0.1 us)
Async XLA Ops:
  7.2 122.6 %copy-start = (f32[512,64]{0,1:T(8,128)S(1)}, f32[512,64]{0,1:T(8,128)}, u32[]{:S(2)}) copy-start(f32[512,64]{0,1:T(8,128)} %param.19) | copy-start | bytes 393220
  7.2 12.0 %copy-start.1 = (bf16[1,512,512]{2,1,0:T(8,128)(2,1)S(1)}, bf16[1,512,512]{2,1,0:T(8,128)(2,1)}, u32[]{:S(2)}) copy-start(bf16[1,512,512]{2,1,0:T(8,128)(2,1)} %param.10) | copy-start | bytes 1572868
  10.4 24.2 %all-to-all-start = ((bf16[8,8,512]{2,1,0:T(8,128)(2,1)}), bf16[8,8,512]{2,1,0:T(8,128)(2,1)S(1)}, u32[]{:S(2)}, u32[]{:S(2)}) async-start(bf16[8,8,512]{2,1,0:T(8,128)(2,1)} %bitcast.5), calls=%async_computation | async-start | bytes 131072 | tf_op jit(solution)/shard_map/all_to_all | solution.py:31
  17.7 112.1 %reduce-scatter.2.cloned.1.call-start = ((), (), s32[]{:S(2)}) async-start(), calls=%async_computation.2 | async-start | bytes 2359296 | tf_op jit(solution)/shard_map/reduce_scatter | solution.py:56
  19.1 9.2 %copy-start.8 = (bf16[1024,512]{1,0:T(8,128)(2,1)S(1)}, bf16[1024,512]{1,0:T(8,128)(2,1)}, u32[]{:S(2)}) copy-start(bf16[1024,512]{1,0:T(8,128)(2,1)} %param.17) | copy-start | bytes 3145732
  28.4 2.0 copy-start.2
  42.2 4.3 %copy-start.10 = (s32[1,2048]{1,0:T(1,128)S(1)}, s32[1,2048]{1,0:T(1,128)}, u32[]{:S(2)}) copy-start(s32[1,2048]{1,0:T(1,128)} %param.13) | copy-start | bytes 24580
  46.5 8.2 %copy-start.5 = (f32[512,512]{1,0:T(8,128)S(1)}, f32[512,512]{1,0:T(8,128)}, u32[]{:S(2)}) copy-start(f32[512,512]{1,0:T(8,128)} %fusion.12) | copy-start | bytes 3145732
  46.5 8.2 %copy-start.9 = (bf16[1024,512]{1,0:T(8,128)(2,1)S(1)}, bf16[1024,512]{1,0:T(8,128)(2,1)}, u32[]{:S(2)}) copy-start(bf16[1024,512]{1,0:T(8,128)(2,1)} %param.17) | copy-start | bytes 3145732
  59.8 69.9 %copy-start.3 = (f32[1,128,512]{2,1,0:T(8,128)S(1)}, f32[1,128,512]{2,1,0:T(8,128)}, u32[]{:S(2)}) copy-start(f32[1,128,512]{2,1,0:T(8,128)} %param.18) | copy-start | bytes 786436
  59.9 253.0 %all-reduce.2.cloned.1.call-start = ((), (), s32[]{:S(2)}) async-start(), calls=%async_computation.3 | async-start | bytes 262144 | tf_op jit(solution)/shard_map/psum | solution.py:66
  129.7 184.5 %copy-start.4 = (f32[128,512]{1,0:T(8,128)S(1)}, f32[128,512]{1,0:T(8,128)}, u32[]{:S(2)}) copy-start(f32[128,512]{1,0:T(8,128)} %reduce-scatter.2.cloned.1.call-done) | copy-start | bytes 786436
  313.8 1.2 copy-start.7
  314.3 0.8 copy-start.6
Sparse Core Ops, SparseCore 0:
  60.0 69.7 reduce-scatter.1
  191.0 121.8 all-reduce.1
where the time goes:
time: 322 us
  waiting for transfers between devices  192 us (60%)
  blocking collectives  45.1 us (14%)
  matrix products  25.9 us (8%)
  local copies, waits for them, and re-layouts  19.9 us (6%)
  other arithmetic  17.5 us (5%)
  between operations  14.2 us (4%)
  starting transfers between devices  7.36 us (2%)
    psum x1, waiting for transfers between devices, body(): new_q = lax.psum(right_part, ('graph', 'dp')) / lax.axis_size('dp')  122 us
    reduce_scatter x1, waiting for transfers between devices, body(): mine = lax.psum_scatter(gradient, 'graph', scatter_dimension=0, tiled=True)  69.8 us
    psum x1, blocking collectives, body(): gram = lax.psum(jnp.dot(own_left.T, own_left, precision=highest), 'graph')  34.8 us
    psum x1, blocking collectives, body(): own_left = lax.psum(local_left, 'dp')  10.3 us
    gather x1, local copies, waits for them, and re-layouts, body(): receiver_rows = node_block[receivers[0]]  9.2 us
    dot_general x1, matrix products, body(): jnp.dot(incidence, edge_new, preferred_element_type=jnp.float32)  8.16 us
    gather x1, local copies, waits for them, and re-layouts, body(): sender_rows = lookup[senders[0]]  7.54 us
    all_to_all x1, starting transfers between devices, body(): lax.all_to_all(outgoing, 'graph', split_axis=0, concat_axis=0, tiled=True)  7.28 us
  transfers between devices with their start and end apart: 3, of which 2 were waited for; matrix products, arithmetic and copies ran while one was open for 5% of the time, Pallas kernels for 0%

commit v1 on v0

v1 whole, which is shorter than its diff:
```python
import functools

import jax
import jax.numpy as jnp
from jax import lax
from jax.experimental import pallas as pl
from jax.experimental.pallas import tpu as pltpu
from jax.sharding import PartitionSpec as P

F32 = jnp.float32
BF16 = jnp.bfloat16
HIGHEST = lax.Precision.HIGHEST
MIB = 1 << 20


def dot_nn(a, b, precision=None):
    return lax.dot_general(
        a, b, (((1,), (0,)), ((), ())), precision=precision, preferred_element_type=F32
    )


def dot_nt(a, b, precision=None):
    return lax.dot_general(
        a, b, (((1,), (1,)), ((), ())), precision=precision, preferred_element_type=F32
    )


def dot_tn(a, b, precision=None):
    return lax.dot_general(
        a, b, (((0,), (0,)), ((), ())), precision=precision, preferred_element_type=F32
    )


def sigmoid(v):
    return 0.5 * jnp.tanh(0.5 * v) + 0.5


def columns_of(row):
    return jnp.broadcast_to(row, (128, row.shape[1])).T


def one_hot_rows(cols, first, width):
    lane = lax.broadcasted_iota(jnp.int32, cols.shape, 1)
    parts = []
    for start in range(0, width, 128):
        size = min(128, width - start)
        hit = jnp.where(cols == lane + (first + start), 1.0, 0.0).astype(BF16)
        parts.append(hit[:, :size])
    return parts[0] if len(parts) == 1 else jnp.concatenate(parts, axis=1)


def pick_kernel(index_ref, node_ref, out_ref):
    nodes = node_ref.shape[0]
    count = index_ref.shape[1]
    row = lax.broadcasted_iota(jnp.int32, (nodes, count), 0)
    hit = jnp.where(row == index_ref[...], 1.0, 0.0).astype(BF16)
    out_ref[...] = dot_tn(hit, node_ref[...]).astype(BF16)


def edge_kernel(edge_ref, send_ref, recv_ref, node_ref, weight_ref, out_ref, table):
    nodes, features = node_ref.shape

    @pl.when(pl.program_id(0) == 0)
    def _():
        node = node_ref[...]
        table[0:features, :] = weight_ref[0:features, :]
        own = dot_nn(node, weight_ref[features : 2 * features, :])
        table[features : features + nodes, :] = own.astype(BF16)
        into = dot_nn(node, weight_ref[2 * features : 3 * features, :])
        table[features + nodes :, :] = into.astype(BF16)

    left = jnp.concatenate(
        [
            edge_ref[...],
            one_hot_rows(columns_of(send_ref[...]), 0, nodes),
            one_hot_rows(columns_of(recv_ref[...]), 0, nodes),
        ],
        axis=1,
    )
    out_ref[...] = dot_nn(left, table[...])


def node_kernel(
    pre_ref,
    edge_ref,
    send_ref,
    recv_ref,
    halo_ref,
    weight_ref,
    node_ref,
    cot_ref,
    wnode_ref,
    new_ref,
    grad_ref,
    table,
    total,
):
    nodes = node_ref.shape[0]
    halo = halo_ref.shape[0]

    @pl.when(pl.program_id(0) == 0)
    def _():
        table[...] = dot_nn(halo_ref[...], weight_ref[...]).astype(BF16)
        total[...] = jnp.zeros_like(total)

    hot = one_hot_rows(columns_of(send_ref[...]), nodes, halo)
    pre = pre_ref[...] + dot_nn(hot, table[...])
    edge_new = (edge_ref[...].astype(F32) + pre * sigmoid(pre)).astype(BF16)
    row = lax.broadcasted_iota(jnp.int32, (nodes, recv_ref.shape[1]), 0)
    incidence = jnp.where(row == recv_ref[...], 1.0, 0.0).astype(BF16)
    total[...] += dot_nn(incidence, edge_new)

    @pl.when(pl.program_id(0) == pl.num_programs(0) - 1)
    def _():
        node = node_ref[...]
        joined = jnp.concatenate([node, total[...].astype(BF16)], axis=1)
        node_pre = dot_nn(joined, wnode_ref[...])
        gate = sigmoid(node_pre)
        new_ref[...] = (node.astype(F32) + node_pre * gate).astype(BF16)
        delta = cot_ref[...].astype(F32) * (gate * (1.0 + node_pre * (1.0 - gate)))
        grad_ref[...] = dot_tn(joined, delta.astype(BF16)).astype(BF16)


def matrix_kernel(got_ref, error_ref, warm_ref, matrix_ref, left_ref):
    matrix = error_ref[...]
    for part in range(got_ref.shape[0]):
        matrix = matrix + got_ref[part].astype(F32)
    matrix_ref[...] = matrix
    left_ref[...] = dot_nt(warm_ref[...], matrix, HIGHEST)


def right_kernel(left_ref, matrix_ref, right_ref):
    right_ref[...] = dot_nn(left_ref[...], matrix_ref[...], HIGHEST)


def inverse_factor(gram, group=8):
    rank = gram.shape[0]
    row = lax.broadcasted_iota(jnp.int32, (rank, rank), 0)
    col = lax.broadcasted_iota(jnp.int32, (rank, rank), 1)
    work = jnp.concatenate([gram, jnp.where(row == col, 1.0, 0.0)], axis=1)
    wide = work.shape[1]
    row = lax.broadcasted_iota(jnp.int32, (rank, wide), 0)
    scale = jnp.ones((rank, wide), F32)
    for start in range(0, rank, group):
        cols = [
            jnp.broadcast_to(work[:, start + j : start + j + 1], (rank, wide))
            for j in range(group)
        ]
        for j in range(group):
            k = start + j
            pivot = jnp.broadcast_to(cols[j][k : k + 1, :], (rank, wide))
            factor = jnp.where(row > k, cols[j] / pivot, 0.0)
            scale = jnp.where(row == k, lax.rsqrt(pivot), scale)
            work = work - factor * work[k : k + 1, :]
            for i in range(j + 1, group):
                cols[i] = cols[i] - factor * cols[i][k : k + 1, :]
    return (work * scale)[:, rank:]


def final_kernel(right_ref, left_ref, matrix_ref, warm_ref, q_ref, update_ref, error_ref, *, groups):
    right = right_ref[...]
    gram = dot_nt(right, warm_ref[...], HIGHEST)
    inverse = inverse_factor(gram)
    ortho = dot_nn(inverse, left_ref[...], HIGHEST)
    new_q = dot_nn(inverse, right, HIGHEST) / groups
    update = dot_tn(ortho, new_q, HIGHEST)
    q_ref[...] = new_q
    update_ref[...] = update
    error_ref[...] = matrix_ref[...] - update


def exchange(x, axes, size, mask):
    return lax.ppermute(x, axes, [(i, i ^ mask) for i in range(size)])


def body(
    node_state,
    edge_state,
    senders,
    receivers,
    send_index,
    cotangent,
    w_edge,
    w_node,
    error_memory,
    warm_q,
):
    node_block = node_state[0]
    edge_block = edge_state[0]
    nodes, features = node_block.shape
    edges = edge_block.shape[0]
    partitions = lax.axis_size("graph")
    replicas = lax.axis_size("dp")
    rank = warm_q.shape[1]
    warm = warm_q.T
    tile = 256
    steps = edges // tile
    params = functools.partial(pltpu.CompilerParams, vmem_limit_bytes=32 * MIB)

    outgoing = pl.pallas_call(
        pick_kernel,
        out_shape=jax.ShapeDtypeStruct((send_index.shape[2], features), BF16),
        compiler_params=params(),
    )(send_index[0], node_block)
    incoming = lax.all_to_all(
        outgoing.reshape(partitions, -1, features), "graph", split_axis=0, concat_axis=0, tiled=True
    ).reshape(-1, features)

    whole = lambda shape: pl.BlockSpec(shape, lambda i: (0,) * len(shape))
    edge_pre = pl.pallas_call(
        edge_kernel,
        grid=(steps,),
        in_specs=[
            pl.BlockSpec((tile, features), lambda i: (i, 0)),
            pl.BlockSpec((1, tile), lambda i: (0, i)),
            pl.BlockSpec((1, tile), lambda i: (0, i)),
            whole(node_block.shape),
            whole(w_edge.shape),
        ],
        out_specs=pl.BlockSpec((tile, features), lambda i: (i, 0)),
        out_shape=jax.ShapeDtypeStruct((edges, features), F32),
        scratch_shapes=[pltpu.VMEM((features + 2 * nodes, features), BF16)],
        compiler_params=params(),
    )(edge_block, senders, receivers, node_block, w_edge)

    new_block, gradient = pl.pallas_call(
        node_kernel,
        grid=(steps,),
        in_specs=[
            pl.BlockSpec((tile, features), lambda i: (i, 0)),
            pl.BlockSpec((tile, features), lambda i: (i, 0)),
            pl.BlockSpec((1, tile), lambda i: (0, i)),
            pl.BlockSpec((1, tile), lambda i: (0, i)),
            whole(incoming.shape),
            pl.BlockSpec((features, features), lambda i: (1, 0)),
            whole(node_block.shape),
            whole(node_block.shape),
            whole(w_node.shape),
        ],
        out_specs=[whole(node_block.shape), whole(w_node.shape)],
        out_shape=[
            jax.ShapeDtypeStruct(node_block.shape, BF16),
            jax.ShapeDtypeStruct(w_node.shape, BF16),
        ],
        scratch_shapes=[
            pltpu.VMEM(incoming.shape, BF16),
            pltpu.VMEM((nodes, features), F32),
        ],
        compiler_params=params(),
    )(
        edge_pre,
        edge_block,
        senders,
        receivers,
        incoming,
        w_edge,
        node_block,
        cotangent[0],
        w_node,
    )

    rows = w_node.shape[0] // partitions
    got = lax.all_to_all(
        gradient.reshape(partitions, rows, features),
        "graph",
        split_axis=0,
        concat_axis=0,
        tiled=True,
    )
    matrix, left = pl.pallas_call(
        matrix_kernel,
        out_shape=[
            jax.ShapeDtypeStruct((rows, features), F32),
            jax.ShapeDtypeStruct((rank, rows), F32),
        ],
        compiler_params=params(),
    )(got, error_memory[0], warm)
    mask = 1
    while mask < replicas:
        left = left + exchange(left, "dp", replicas, mask)
        mask *= 2

    right = pl.pallas_call(
        right_kernel,
        out_shape=jax.ShapeDtypeStruct((rank, features), F32),
        compiler_params=params(),
    )(left, matrix)
    side = lax.axis_index("dp") % 2
    half = rank // 2
    low, high = right[:half], right[half:]
    kept = jnp.where(side == 0, low, high)
    given = jnp.where(side == 0, high, low)
    kept = kept + exchange(given, "dp", replicas, 1)
    mask = 2
    while mask < replicas:
        kept = kept + exchange(kept, "dp", replicas, mask)
        mask *= 2
    mask = 1
    while mask < partitions:
        kept = kept + exchange(kept, "graph", partitions, mask)
        mask *= 2
    other = exchange(kept, "dp", replicas, 1)
    right = jnp.concatenate(
        [jnp.where(side == 0, kept, other), jnp.where(side == 0, other, kept)], axis=0
    )

    new_q, update, new_error = pl.pallas_call(
        functools.partial(final_kernel, groups=replicas),
        out_shape=[
            jax.ShapeDtypeStruct((rank, features), F32),
            jax.ShapeDtypeStruct((rows, features), F32),
            jax.ShapeDtypeStruct((rows, features), F32),
        ],
        compiler_params=params(),
    )(right, left, matrix, warm)
    return (new_block[None], update, new_error[None], new_q.T)


def solution(mesh):
    return jax.shard_map(
        body,
        mesh=mesh,
        in_specs=(
            P("dp", "graph", None),
            P("dp", "graph", None),
            P("dp", "graph"),
            P("dp", "graph"),
            P("dp", "graph", None),
            P("dp", "graph", None),
            P(),
            P(),
            P("dp", "graph", None),
            P(),
        ),
        out_specs=(P("dp", "graph", None), P("graph", None), P("dp", "graph", None), P()),
        check_vma=False,
    )
```

time: 322 us -> 98.3 us (0.31)
  waiting for transfers between devices: 192 us -> 19 us
  matrix products: 25.9 us -> 0 us
  Pallas kernels: 0 us -> 18.4 us
  other arithmetic: 17.5 us -> 0.1 us
  blocking collectives: 45.1 us -> 31.2 us
  between operations: 14.2 us -> 0.79 us
  starting transfers between devices: 7.36 us -> 14.3 us
  local copies, waits for them, and re-layouts: 19.9 us -> 13.9 us
    psum x1 -> x0, waiting for transfers between devices: 122 us -> none  [body(): new_q = lax.psum(right_part, ('graph', 'dp')) / lax.axis_size('dp')]
    reduce_scatter x1 -> x0, waiting for transfers between devices: 69.8 us -> none  [body(): mine = lax.psum_scatter(gradient, 'graph', scatter_dimension=0, tiled=True)]
    psum x2 -> x0, blocking collectives: 45.1 us -> none  [the longest x1 34.8 us: body(): gram = lax.psum(jnp.dot(own_left.T, own_left, precision=highest), 'graph')]
    all_to_all x0 -> x1, blocking collectives: none -> 31.2 us  [body(): lax.all_to_all(gradient.reshape(partitions, rows, features), 'graph', spl...]
    dot_general x11 -> x0, matrix products: 25.7 us -> none  [the longest x1 8.16 us: body(): jnp.dot(incidence, edge_new, preferred_element_type=jnp.float32)]
    gather x3 -> x0, local copies, waits for them, and re-layouts: 19.2 us -> none  [the longest x1 9.2 us: body(): receiver_rows = node_block[receivers[0]]]
    ppermute x0 -> x8, waiting for transfers between devices: none -> 19 us  [exchange(): return lax.ppermute(x, axes, [(i, i ^ mask) for i in range(size)])]
    pallas_call x0 -> x6, Pallas kernels: none -> 18.4 us  [the longest x1 7.71 us: body(): pl.pallas_call(node_kernel, grid=(steps,), in_specs=[pl.BlockSpec((tile,...]
  transfers between devices with their start and end apart: 3 -> 9, of which waited for: 2 -> 8; matrix products, arithmetic and copies ran while one was open for 5% -> 0% of each run, Pallas kernels for 0% -> 6%
where the time goes in v1:
time: 98.3 us; the launch traced here: 97.7 us
  blocking collectives  31.2 us (32%)
  waiting for transfers between devices  19 us (19%)
  Pallas kernels  18.4 us (19%)
  starting transfers between devices  14.3 us (15%)
  local copies, waits for them, and re-layouts  13.9 us (14%)
    all_to_all x1, blocking collectives, body(): lax.all_to_all(gradient.reshape(partitions, rows, features), 'graph', spl...  31.2 us
    ppermute x8, waiting for transfers between devices, exchange(): return lax.ppermute(x, axes, [(i, i ^ mask) for i in range(size)])  19 us
    unnamed x36, local copies, waits for them, and re-layouts  13.9 us
    pallas_call x1, Pallas kernels, body(): pl.pallas_call(node_kernel, grid=(steps,), in_specs=[pl.BlockSpec((tile,...  7.71 us
    all_to_all x1, starting transfers between devices, body(): lax.all_to_all(outgoing.reshape(partitions, -1, features), 'graph', split...  7.28 us
    ppermute x8, starting transfers between devices, exchange(): return lax.ppermute(x, axes, [(i, i ^ mask) for i in range(size)])  7 us
    pallas_call x1, Pallas kernels, body(): pl.pallas_call(edge_kernel, grid=(steps,), in_specs=[pl.BlockSpec((tile,...  5.43 us
    pallas_call x1, Pallas kernels, body(): pl.pallas_call(functools.partial(final_kernel, groups=replicas), out_shap...  3.65 us
  transfers between devices with their start and end apart: 9, of which 8 were waited for; matrix products, arithmetic and copies ran while one was open for 0% of the time, Pallas kernels for 6%

profile of v1, /device:TPU:0, one launch (start us, length us, event | category | flops | bytes accessed | tf_op | source)
XLA Modules:
  0.0 97.7 jit_solution(1549552256329257736)
XLA Ops:
  0.6 0.0 copy-start.6
  0.6 1.0 %copy-done.6 = bf16[1,512,512]{2,1,0:T(8,128)(2,1)S(1)} copy-done((bf16[1,512,512]{2,1,0:T(8,128)(2,1)S(1)}, bf16[1,512,512]{2,1,0:T(8,128)(2,1)}, u32[]{:S(2)}) %copy-start.6) | copy-done | bytes 524312
  1.7 0.0 copy-start.17
  1.7 0.7 copy-done.17
  2.3 0.9 shard_map.130
  3.2 7.3 %all-to-all-start = ((bf16[8,8,512]{2,1,0:T(8,128)(2,1)}), bf16[8,8,512]{2,1,0:T(8,128)(2,1)S(1)}, u32[]{:S(2)}, u32[]{:S(2)}) async-start(bf16[8,8,512]{2,1,0:T(8,128)(2,1)} %bitcast.3), calls=%async_computation | async-start | bytes 131072 | tf_op jit(solution)/shard_map/all_to_all | solution.py:205
  10.5 1.6 %copy-done.2 = bf16[1,2048,512]{2,1,0:T(8,128)(2,1)S(1)} copy-done((bf16[1,2048,512]{2,1,0:T(8,128)(2,1)S(1)}, bf16[1,2048,512]{2,1,0:T(8,128)(2,1)}, u32[]{:S(2)}) %copy-start.2) | copy-done | bytes 2097176
  12.1 1.4 %copy-done.4 = bf16[1536,512]{1,0:T(8,128)(2,1)S(1)} copy-done((bf16[1536,512]{1,0:T(8,128)(2,1)S(1)}, bf16[1536,512]{1,0:T(8,128)(2,1)}, u32[]{:S(2)}) %copy-start.4) | copy-done | bytes 1572888
  13.5 1.0 %copy-done.7 = bf16[1,512,512]{2,1,0:T(8,128)(2,1)S(1)} copy-done((bf16[1,512,512]{2,1,0:T(8,128)(2,1)S(1)}, bf16[1,512,512]{2,1,0:T(8,128)(2,1)}, u32[]{:S(2)}) %copy-start.7) | copy-done | bytes 524312
  14.5 0.7 copy-done.13
  15.2 0.7 copy-done.15
  15.9 0.0 copy-start.16
  15.9 5.4 %shard_map.129.pre_ref = f32[2048,512]{1,0:T(8,128)S(1)} custom-call(bf16[2048,512]{1,0:T(8,128)(2,1)S(1)} %bitcast.12, s32[1,2048]{1,0:T(1,128)S(1)} %copy-done.13, s32[1,2048]{1,0:T(1,128)S(1)} %copy-done.15, bf16[512,512]{1,0:T(8,128)(2,1)S(1)} %bitcast.15, bf16[1536,512]{1,0:T(8,128)(2,1)S(1)} %copy-done.4), custom_call_target="tpu_custom_call" | custom-call | tf_op jit(solution)/shard_map/pallas_call | solution.py:210
  21.4 0.0 copy-start
  21.4 2.0 %copy-done = f32[2048,512]{1,0:T(8,128)} copy-done((f32[2048,512]{1,0:T(8,128)}, f32[2048,512]{1,0:T(8,128)S(1)}, u32[]{:S(2)}) %copy-start) | copy-done | bytes 4194328
  23.3 0.0 all-to-all-done
  23.3 0.0 copy-done.3
  23.3 0.0 copy-done.8
  23.3 0.0 copy-done.10
  23.4 0.0 copy-done.14
  23.4 0.0 copy-done.16
  23.4 0.0 copy-start.1
  23.4 2.2 %copy-done.1 = f32[2048,512]{1,0:T(8,128)S(1)} copy-done((f32[2048,512]{1,0:T(8,128)S(1)}, f32[2048,512]{1,0:T(8,128)}, u32[]{:S(2)}) %copy-start.1) | copy-done | bytes 4194328
  25.6 1.4 %copy-done.5 = bf16[1536,512]{1,0:T(8,128)(2,1)S(1)} copy-done((bf16[1536,512]{1,0:T(8,128)(2,1)S(1)}, bf16[1536,512]{1,0:T(8,128)(2,1)}, u32[]{:S(2)}) %copy-start.5) | copy-done | bytes 1572888
  27.0 1.2 %copy-done.9 = bf16[1024,512]{1,0:T(8,128)(2,1)S(1)} copy-done((bf16[1024,512]{1,0:T(8,128)(2,1)S(1)}, bf16[1024,512]{1,0:T(8,128)(2,1)}, u32[]{:S(2)}) %copy-start.9) | copy-done | bytes 1048600
  28.2 7.7 %shard_map.131 = (bf16[512,512]{1,0:T(8,128)(2,1)}, bf16[1024,512]{1,0:T(8,128)(2,1)S(1)}) custom-call(f32[2048,512]{1,0:T(8,128)S(1)} %copy-done.1, bf16[2048,512]{1,0:T(8,128)(2,1)S(1)} %bitcast.13, s32[1,2048]{1,0:T(1,128)S(1)} %copy-done.14, s32[1,2048]{1,0:T(1,128)S(1)} %copy-done.16, bf16[64,512]{1,0:T(8,128)(2,1)S(1)} %bitcast.21, ...), custom_call_target="tpu_custom_call" | custom-call | tf_op jit(solution)/shard_map/pallas_call | solution.py:226
  35.9 31.2 %all_to_all.10.got_ref = bf16[8,128,512]{2,1,0:T(8,128)(2,1)S(1)} all-to-all(bf16[8,128,512]{2,1,0:T(8,128)(2,1)S(1)} %bitcast.17), channel_id=1, replica_groups=mesh['graph'=8,'dp'=4] {'graph'}, dimensions={0} | all-to-all | bytes 2097152 | tf_op jit(solution)/shard_map/all_to_all | solution.py:263
  67.1 0.0 copy-done.11
  67.1 0.0 copy-done.12
  67.1 0.5 shard_map.132
  67.6 0.1 collective-permute-start
  67.7 1.2 %collective-permute-done = f32[64,128]{1,0:T(8,128)S(1)} collective-permute-done((f32[64,128]{1,0:T(8,128)S(1)}, f32[64,128]{1,0:T(8,128)S(1)}, u32[]{:S(2)}, u32[]{:S(2)}) %collective-permute-start) | collective-permute-done | bytes 32800 | tf_op jit(solution)/shard_map/ppermute | solution.py:173
  68.9 1.5 %collective-permute-start.1 = (f32[64,128]{1,0:T(8,128)S(1)}, f32[64,128]{1,0:T(8,128)S(1)}, u32[]{:S(2)}, u32[]{:S(2)}) collective-permute-start(f32[64,128]{1,0:T(8,128)S(1)} %add.26), channel_id=1, source_target_pairs={{0,2},{1,3},{2,0},{3,1},{4,6},{5,7},{6,4},{7,5},{8,10},{9,11},{10,... | collective-permute-start | bytes 98312 | tf_op jit(solution)/shard_map/ppermute | solution.py:173
  70.4 2.4 %collective-permute-done.1 = f32[64,128]{1,0:T(8,128)S(1)} collective-permute-done((f32[64,128]{1,0:T(8,128)S(1)}, f32[64,128]{1,0:T(8,128)S(1)}, u32[]{:S(2)}, u32[]{:S(2)}) %collective-permute-start.1) | collective-permute-done | bytes 32800 | tf_op jit(solution)/shard_map/ppermute | solution.py:173
  72.8 0.3 shard_map.133
  73.1 0.1 collective-permute-start.2
  73.2 1.2 %collective-permute-done.2 = f32[32,512]{1,0:T(8,128)S(1)} collective-permute-done((f32[32,512]{1,0:T(8,128)S(1)}, f32[32,512]{1,0:T(8,128)S(1)}, u32[]{:S(2)}, u32[]{:S(2)}) %collective-permute-start.2) | collective-permute-done | bytes 65568 | tf_op jit(solution)/shard_map/ppermute | solution.py:173
  74.4 1.6 %collective-permute-start.3 = (f32[32,512]{1,0:T(8,128)S(1)}, f32[32,512]{1,0:T(8,128)S(1)}, u32[]{:S(2)}, u32[]{:S(2)}) collective-permute-start(f32[32,512]{1,0:T(8,128)S(1)} %select_add_fusion), channel_id=1, source_target_pairs={{0,2},{1,3},{2,0},{3,1},{4,6},{5,7},{6,4},{7,5},{8,10},{9,11},{10,... | collective-permute-start | bytes 196616 | tf_op jit(solution)/shard_map/ppermute | solution.py:173
  76.0 2.7 %collective-permute-done.3 = f32[32,512]{1,0:T(8,128)S(1)} collective-permute-done((f32[32,512]{1,0:T(8,128)S(1)}, f32[32,512]{1,0:T(8,128)S(1)}, u32[]{:S(2)}, u32[]{:S(2)}) %collective-permute-start.3) | collective-permute-done | bytes 65568 | tf_op jit(solution)/shard_map/ppermute | solution.py:173
  78.8 1.5 %collective-permute-start.4 = (f32[32,512]{1,0:T(8,128)S(1)}, f32[32,512]{1,0:T(8,128)S(1)}, u32[]{:S(2)}, u32[]{:S(2)}) collective-permute-start(f32[32,512]{1,0:T(8,128)S(1)} %add.29), channel_id=1, source_target_pairs={{0,4},{4,0},{8,12},{12,8},{16,20},{20,16},{24,28},{28,24},{1,5},{5... | collective-permute-start | bytes 196616 | tf_op jit(solution)/shard_map/ppermute | solution.py:173
  80.3 2.9 %collective-permute-done.4 = f32[32,512]{1,0:T(8,128)S(1)} collective-permute-done((f32[32,512]{1,0:T(8,128)S(1)}, f32[32,512]{1,0:T(8,128)S(1)}, u32[]{:S(2)}, u32[]{:S(2)}) %collective-permute-start.4) | collective-permute-done | bytes 65568 | tf_op jit(solution)/shard_map/ppermute | solution.py:173
  83.1 1.1 %collective-permute-start.5 = (f32[32,512]{1,0:T(8,128)S(1)}, f32[32,512]{1,0:T(8,128)S(1)}, u32[]{:S(2)}, u32[]{:S(2)}) collective-permute-start(f32[32,512]{1,0:T(8,128)S(1)} %add.30), channel_id=1, source_target_pairs={{0,8},{4,12},{8,0},{12,4},{16,24},{20,28},{24,16},{28,20},{1,9},{5... | collective-permute-start | bytes 196616 | tf_op jit(solution)/shard_map/ppermute | solution.py:173
  84.3 3.2 %collective-permute-done.5 = f32[32,512]{1,0:T(8,128)S(1)} collective-permute-done((f32[32,512]{1,0:T(8,128)S(1)}, f32[32,512]{1,0:T(8,128)S(1)}, u32[]{:S(2)}, u32[]{:S(2)}) %collective-permute-start.5) | collective-permute-done | bytes 65568 | tf_op jit(solution)/shard_map/ppermute | solution.py:173
  87.5 1.1 %collective-permute-start.6 = (f32[32,512]{1,0:T(8,128)S(1)}, f32[32,512]{1,0:T(8,128)S(1)}, u32[]{:S(2)}, u32[]{:S(2)}) collective-permute-start(f32[32,512]{1,0:T(8,128)S(1)} %add.31), channel_id=1, source_target_pairs={{0,16},{4,20},{8,24},{12,28},{16,0},{20,4},{24,8},{28,12},{1,17},{... | collective-permute-start | bytes 196616 | tf_op jit(solution)/shard_map/ppermute | solution.py:173
  88.5 4.1 %collective-permute-done.6 = f32[32,512]{1,0:T(8,128)S(1)} collective-permute-done((f32[32,512]{1,0:T(8,128)S(1)}, f32[32,512]{1,0:T(8,128)S(1)}, u32[]{:S(2)}, u32[]{:S(2)}) %collective-permute-start.6) | collective-permute-done | bytes 65568 | tf_op jit(solution)/shard_map/ppermute | solution.py:173
  92.7 0.1 collective-permute-start.7
  92.8 1.2 %collective-permute-done.7 = f32[32,512]{1,0:T(8,128)S(1)} collective-permute-done((f32[32,512]{1,0:T(8,128)S(1)}, f32[32,512]{1,0:T(8,128)S(1)}, u32[]{:S(2)}, u32[]{:S(2)}) %collective-permute-start.7) | collective-permute-done | bytes 65568 | tf_op jit(solution)/shard_map/ppermute | solution.py:173
  94.1 3.6 %shard_map.134 = (f32[64,512]{1,0:T(8,128)}, f32[128,512]{1,0:T(8,128)}, f32[128,512]{1,0:T(8,128)}) custom-call(f32[64,512]{1,0:T(8,128)S(1)} %pad_maximum_fusion.right_ref, f32[64,128]{1,0:T(8,128)S(1)} %add.27.left_ref, f32[128,512]{1,0:T(8,128)S(1)} %get-tuple-element.14.matrix_ref, f32[64,512]{1,0:T(8,128)S(1)} %bitcast.20), custom_call_target="tpu_custom_call" | custom-call | tf_op jit(solution)/shard_map/pallas_call | solution.py:307
  (23 shorter events, 0.1 us)
Async XLA Ops:
  0.6 1.0 %copy-start.6 = (bf16[1,512,512]{2,1,0:T(8,128)(2,1)S(1)}, bf16[1,512,512]{2,1,0:T(8,128)(2,1)}, u32[]{:S(2)}) copy-start(bf16[1,512,512]{2,1,0:T(8,128)(2,1)} %param.10) | copy-start | bytes 1572868
  1.7 0.7 copy-start.17
  3.2 20.1 %all-to-all-start = ((bf16[8,8,512]{2,1,0:T(8,128)(2,1)}), bf16[8,8,512]{2,1,0:T(8,128)(2,1)S(1)}, u32[]{:S(2)}, u32[]{:S(2)}) async-start(bf16[8,8,512]{2,1,0:T(8,128)(2,1)} %bitcast.3), calls=%async_computation | async-start | bytes 131072 | tf_op jit(solution)/shard_map/all_to_all | solution.py:205
  10.5 1.6 %copy-start.2 = (bf16[1,2048,512]{2,1,0:T(8,128)(2,1)S(1)}, bf16[1,2048,512]{2,1,0:T(8,128)(2,1)}, u32[]{:S(2)}) copy-start(bf16[1,2048,512]{2,1,0:T(8,128)(2,1)} %param.11) | copy-start | bytes 6291460
  12.1 1.4 %copy-start.4 = (bf16[1536,512]{1,0:T(8,128)(2,1)S(1)}, bf16[1536,512]{1,0:T(8,128)(2,1)}, u32[]{:S(2)}) copy-start(bf16[1536,512]{1,0:T(8,128)(2,1)} %weight_ref.3) | copy-start | bytes 4718596
  13.5 1.0 %copy-start.7 = (bf16[1,512,512]{2,1,0:T(8,128)(2,1)S(1)}, bf16[1,512,512]{2,1,0:T(8,128)(2,1)}, u32[]{:S(2)}) copy-start(bf16[1,512,512]{2,1,0:T(8,128)(2,1)} %param.10) | copy-start | bytes 1572868
  14.5 0.7 copy-start.13
  15.2 0.7 copy-start.15
  15.9 7.4 %copy-start.3 = (bf16[1,2048,512]{2,1,0:T(8,128)(2,1)S(1)}, bf16[1,2048,512]{2,1,0:T(8,128)(2,1)}, u32[]{:S(2)}) copy-start(bf16[1,2048,512]{2,1,0:T(8,128)(2,1)} %param.11) | copy-start | bytes 6291460
  15.9 7.4 %copy-start.8 = (bf16[1,512,512]{2,1,0:T(8,128)(2,1)S(1)}, bf16[1,512,512]{2,1,0:T(8,128)(2,1)}, u32[]{:S(2)}) copy-start(bf16[1,512,512]{2,1,0:T(8,128)(2,1)} %param.10) | copy-start | bytes 1572868
  15.9 7.4 %copy-start.10 = (bf16[1,512,512]{2,1,0:T(8,128)(2,1)S(1)}, bf16[1,512,512]{2,1,0:T(8,128)(2,1)}, u32[]{:S(2)}) copy-start(bf16[1,512,512]{2,1,0:T(8,128)(2,1)} %param.15) | copy-start | bytes 1572868
  15.9 7.4 %copy-start.14 = (s32[1,2048]{1,0:T(1,128)S(1)}, s32[1,2048]{1,0:T(1,128)}, u32[]{:S(2)}) copy-start(s32[1,2048]{1,0:T(1,128)} %send_ref.3) | copy-start | bytes 24580
  15.9 7.4 %copy-start.16 = (s32[1,2048]{1,0:T(1,128)S(1)}, s32[1,2048]{1,0:T(1,128)}, u32[]{:S(2)}) copy-start(s32[1,2048]{1,0:T(1,128)} %recv_ref.3) | copy-start | bytes 24580
  21.4 2.0 %copy-start = (f32[2048,512]{1,0:T(8,128)}, f32[2048,512]{1,0:T(8,128)S(1)}, u32[]{:S(2)}) copy-start(f32[2048,512]{1,0:T(8,128)S(1)} %shard_map.129.pre_ref) | copy-start | bytes 12582916
  23.4 2.2 %copy-start.1 = (f32[2048,512]{1,0:T(8,128)S(1)}, f32[2048,512]{1,0:T(8,128)}, u32[]{:S(2)}) copy-start(f32[2048,512]{1,0:T(8,128)} %copy-done) | copy-start | bytes 12582916
  25.6 1.4 %copy-start.5 = (bf16[1536,512]{1,0:T(8,128)(2,1)S(1)}, bf16[1536,512]{1,0:T(8,128)(2,1)}, u32[]{:S(2)}) copy-start(bf16[1536,512]{1,0:T(8,128)(2,1)} %weight_ref.3) | copy-start | bytes 4718596
  27.0 1.2 %copy-start.9 = (bf16[1024,512]{1,0:T(8,128)(2,1)S(1)}, bf16[1024,512]{1,0:T(8,128)(2,1)}, u32[]{:S(2)}) copy-start(bf16[1024,512]{1,0:T(8,128)(2,1)} %wnode_ref.1) | copy-start | bytes 3145732
  35.9 31.2 %copy-start.11 = (f32[512,64]{0,1:T(8,128)S(1)}, f32[512,64]{0,1:T(8,128)}, u32[]{:S(2)}) copy-start(f32[512,64]{0,1:T(8,128)} %param.19) | copy-start | bytes 393220
  35.9 31.2 %copy-start.12 = (f32[1,128,512]{2,1,0:T(8,128)S(1)}, f32[1,128,512]{2,1,0:T(8,128)}, u32[]{:S(2)}) copy-start(f32[1,128,512]{2,1,0:T(8,128)} %param.18) | copy-start | bytes 786436
  67.6 1.3 %collective-permute-start = (f32[64,128]{1,0:T(8,128)S(1)}, f32[64,128]{1,0:T(8,128)S(1)}, u32[]{:S(2)}, u32[]{:S(2)}) collective-permute-start(f32[64,128]{1,0:T(8,128)S(1)} %get-tuple-element.13), channel_id=1, source_target_pairs={{0,1},{1,0},{2,3},{3,2},{4,5},{5,4},{6,7},{7,6},{8,9},{9,8},{10,11... | collective-permute-start | bytes 98312 | tf_op jit(solution)/shard_map/ppermute | solution.py:173
  68.9 3.9 %collective-permute-start.1 = (f32[64,128]{1,0:T(8,128)S(1)}, f32[64,128]{1,0:T(8,128)S(1)}, u32[]{:S(2)}, u32[]{:S(2)}) collective-permute-start(f32[64,128]{1,0:T(8,128)S(1)} %add.26), channel_id=1, source_target_pairs={{0,2},{1,3},{2,0},{3,1},{4,6},{5,7},{6,4},{7,5},{8,10},{9,11},{10,... | collective-permute-start | bytes 98312 | tf_op jit(solution)/shard_map/ppermute | solution.py:173
  73.1 1.3 %collective-permute-start.2 = (f32[32,512]{1,0:T(8,128)S(1)}, f32[32,512]{1,0:T(8,128)S(1)}, u32[]{:S(2)}, u32[]{:S(2)}) collective-permute-start(f32[32,512]{1,0:T(8,128)S(1)} %slice_select_fusion), channel_id=1, source_target_pairs={{0,1},{1,0},{2,3},{3,2},{4,5},{5,4},{6,7},{7,6},{8,9},{9,8},{10,11... | collective-permute-start | bytes 196616 | tf_op jit(solution)/shard_map/ppermute | solution.py:173
  74.4 4.3 %collective-permute-start.3 = (f32[32,512]{1,0:T(8,128)S(1)}, f32[32,512]{1,0:T(8,128)S(1)}, u32[]{:S(2)}, u32[]{:S(2)}) collective-permute-start(f32[32,512]{1,0:T(8,128)S(1)} %select_add_fusion), channel_id=1, source_target_pairs={{0,2},{1,3},{2,0},{3,1},{4,6},{5,7},{6,4},{7,5},{8,10},{9,11},{10,... | collective-permute-start | bytes 196616 | tf_op jit(solution)/shard_map/ppermute | solution.py:173
  78.8 4.3 %collective-permute-start.4 = (f32[32,512]{1,0:T(8,128)S(1)}, f32[32,512]{1,0:T(8,128)S(1)}, u32[]{:S(2)}, u32[]{:S(2)}) collective-permute-start(f32[32,512]{1,0:T(8,128)S(1)} %add.29), channel_id=1, source_target_pairs={{0,4},{4,0},{8,12},{12,8},{16,20},{20,16},{24,28},{28,24},{1,5},{5... | collective-permute-start | bytes 196616 | tf_op jit(solution)/shard_map/ppermute | solution.py:173
  83.1 4.3 %collective-permute-start.5 = (f32[32,512]{1,0:T(8,128)S(1)}, f32[32,512]{1,0:T(8,128)S(1)}, u32[]{:S(2)}, u32[]{:S(2)}) collective-permute-start(f32[32,512]{1,0:T(8,128)S(1)} %add.30), channel_id=1, source_target_pairs={{0,8},{4,12},{8,0},{12,4},{16,24},{20,28},{24,16},{28,20},{1,9},{5... | collective-permute-start | bytes 196616 | tf_op jit(solution)/shard_map/ppermute | solution.py:173
  87.5 5.2 %collective-permute-start.6 = (f32[32,512]{1,0:T(8,128)S(1)}, f32[32,512]{1,0:T(8,128)S(1)}, u32[]{:S(2)}, u32[]{:S(2)}) collective-permute-start(f32[32,512]{1,0:T(8,128)S(1)} %add.31), channel_id=1, source_target_pairs={{0,16},{4,20},{8,24},{12,28},{16,0},{20,4},{24,8},{28,12},{1,17},{... | collective-permute-start | bytes 196616 | tf_op jit(solution)/shard_map/ppermute | solution.py:173
  92.7 1.3 %collective-permute-start.7 = (f32[32,512]{1,0:T(8,128)S(1)}, f32[32,512]{1,0:T(8,128)S(1)}, u32[]{:S(2)}, u32[]{:S(2)}) collective-permute-start(f32[32,512]{1,0:T(8,128)S(1)} %add.32), channel_id=1, source_target_pairs={{0,1},{1,0},{2,3},{3,2},{4,5},{5,4},{6,7},{7,6},{8,9},{9,8},{10,11... | collective-permute-start | bytes 196616 | tf_op jit(solution)/shard_map/ppermute | solution.py:173

commit v2 on v1

v2 whole, which is shorter than its diff:
```python
import functools

import jax
import jax.numpy as jnp
from jax import lax
from jax.experimental import pallas as pl
from jax.experimental.pallas import tpu as pltpu
from jax.sharding import PartitionSpec as P

F32 = jnp.float32
BF16 = jnp.bfloat16
HIGHEST = lax.Precision.HIGHEST
MIB = 1 << 20


def dot_nn(a, b, precision=None):
    return lax.dot_general(
        a, b, (((1,), (0,)), ((), ())), precision=precision, preferred_element_type=F32
    )


def dot_nt(a, b, precision=None):
    return lax.dot_general(
        a, b, (((1,), (1,)), ((), ())), precision=precision, preferred_element_type=F32
    )


def dot_tn(a, b, precision=None):
    return lax.dot_general(
        a, b, (((0,), (0,)), ((), ())), precision=precision, preferred_element_type=F32
    )


def sigmoid(v):
    return 0.5 * jnp.tanh(0.5 * v) + 0.5


def columns_of(row):
    return jnp.broadcast_to(row, (128, row.shape[1])).T


def one_hot_rows(cols, first, width):
    lane = lax.broadcasted_iota(jnp.int32, cols.shape, 1)
    parts = []
    for start in range(0, width, 128):
        size = min(128, width - start)
        hit = jnp.where(cols == lane + (first + start), 1.0, 0.0).astype(BF16)
        parts.append(hit[:, :size])
    return parts[0] if len(parts) == 1 else jnp.concatenate(parts, axis=1)


def pick_kernel(index_hbm, node_hbm, out_ref, index, node, sems):
    copies = [
        pltpu.make_async_copy(index_hbm, index, sems.at[0]),
        pltpu.make_async_copy(node_hbm, node, sems.at[1]),
    ]
    for copy in copies:
        copy.start()
    for copy in copies:
        copy.wait()
    row = lax.broadcasted_iota(jnp.int32, (node.shape[0], index.shape[1]), 0)
    hit = jnp.where(row == index[...], 1.0, 0.0).astype(BF16)
    out_ref[...] = dot_tn(hit, node[...]).astype(BF16)


def layer_kernel(
    place_ref,
    send_ref,
    recv_ref,
    halo_ref,
    edge_hbm,
    node_hbm,
    cot_hbm,
    wedge_hbm,
    wnode_hbm,
    new_ref,
    near_send_ref,
    near_keep_ref,
    far_send_ref,
    far_keep_ref,
    grad,
    edge,
    look,
    weight,
    table,
    total,
    cot,
    joined,
    wnode,
    sems,
    edge_sems,
    *,
    tile,
):
    nodes, features = node_hbm.shape
    halo = halo_ref.shape[0]
    edges = edge_hbm.shape[0]
    steps = edges // tile
    reach = nodes + halo

    def edge_copy(step):
        rows = pl.ds(step * tile, tile)
        return pltpu.make_async_copy(edge_hbm.at[rows, :], edge.at[rows, :], edge_sems.at[step])

    node_copy = pltpu.make_async_copy(node_hbm, look.at[pl.ds(0, nodes), :], sems.at[0])
    weight_copies = [
        pltpu.make_async_copy(
            wedge_hbm.at[pl.ds(part * features, features), :],
            weight.at[pl.ds(part * features, features), :],
            sems.at[1 + part],
        )
        for part in (1, 2, 0)
    ]
    last = [
        pltpu.make_async_copy(wnode_hbm, wnode, sems.at[4]),
        pltpu.make_async_copy(cot_hbm, cot, sems.at[5]),
    ]
    node_copy.start()
    for copy in weight_copies:
        copy.start()
    for step in range(steps):
        edge_copy(step).start()
    for copy in last:
        copy.start()
    look[nodes:, :] = halo_ref[...]
    node_copy.wait()
    joined[:, 0:features] = look[0:nodes, :]
    weight_copies[0].wait()
    own = dot_nn(look[...], weight[features : 2 * features, :])
    table[features : features + reach, :] = (0.5 * own).astype(BF16)
    weight_copies[1].wait()
    into = dot_nn(look[0:nodes, :], weight[2 * features :, :])
    table[features + reach :, :] = (0.5 * into).astype(BF16)
    weight_copies[2].wait()
    table[0:features, :] = weight[0:features, :] * 0.5

    for step in range(steps):
        rows = pl.ds(step * tile, tile)
        edge_copy(step).wait()
        block = edge[rows, :]
        recv = recv_ref[:, rows]
        left = jnp.concatenate(
            [
                block,
                one_hot_rows(columns_of(send_ref[:, rows]), 0, reach),
                one_hot_rows(columns_of(recv), 0, nodes),
            ],
            axis=1,
        )
        half = dot_nn(left, table[...])
        edge_new = (block.astype(F32) + (half + half * jnp.tanh(half))).astype(BF16)
        row = lax.broadcasted_iota(jnp.int32, (nodes, tile), 0)
        incidence = jnp.where(row == recv, 1.0, 0.0).astype(BF16)
        part = dot_nn(incidence, edge_new)
        if step == 0:
            total[...] = part
        else:
            total[...] += part

    joined[:, features:] = total[...].astype(BF16)
    for copy in last:
        copy.wait()
    block = 128
    for step in range(nodes // block):
        rows = pl.ds(step * block, block)
        half = 0.5 * dot_nn(joined[rows, :], wnode[...])
        turn = jnp.tanh(half)
        node = joined[rows, 0:features].astype(F32)
        new_ref[rows, :] = (node + (half + half * turn)).astype(BF16)
        slope = (0.5 + 0.5 * turn) * (1.0 + half * (1.0 - turn))
        look[rows, :] = (cot[rows, :].astype(F32) * slope).astype(BF16)
    grad[...] = dot_tn(joined[...], look[0:nodes, :])
    me = place_ref[0]
    side = place_ref[1]
    parts, size, width = near_keep_ref.shape
    bits = (2 * parts).bit_length() - 1
    for refs, order, turn in (
        ((near_keep_ref, near_send_ref), stage_order(bits, False), side),
        ((far_keep_ref, far_send_ref), stage_order(bits, True), 1 - side),
    ):
        column = pl.multiple_of(turn * width, width)
        for slot in range(2 * parts):
            offset = 0
            for stage, bit in enumerate(order):
                offset |= ((slot >> (bits - 1 - stage)) & 1) << bit
            row = pl.multiple_of((me ^ offset) * size, size)
            block = grad[pl.ds(row, size), pl.ds(column, width)]
            ref = refs[slot // parts]
            ref[slot % parts] = block.astype(ref.dtype)


def matrix_kernel(place_ref, keep_ref, got_ref, error_ref, near_ref, far_ref):
    width = near_ref.shape[1]
    for half, (out_ref, turn) in enumerate(
        ((near_ref, place_ref[1]), (far_ref, 1 - place_ref[1]))
    ):
        column = pl.multiple_of(turn * width, width)
        out_ref[...] = (
            keep_ref[half, 0] + got_ref[half, 0].astype(F32) + error_ref[:, pl.ds(column, width)]
        )


def left_kernel(place_ref, mean_ref, got_ref, warm_ref, sum_ref, left_ref):
    width = mean_ref.shape[1]
    total = mean_ref[...] + got_ref[...].astype(F32)
    sum_ref[...] = total
    column = pl.multiple_of(place_ref[1] * width, width)
    left_ref[...] = dot_nt(warm_ref[:, pl.ds(column, width)], total, HIGHEST)


def right_kernel(left_ref, other_ref, sum_ref, full_ref, right_ref):
    left = left_ref[...] + other_ref[...]
    full_ref[...] = left
    right_ref[...] = dot_nn(left, sum_ref[...], HIGHEST)


def inverse_factor(gram, group=8):
    rank = gram.shape[0]
    row = lax.broadcasted_iota(jnp.int32, (rank, rank), 0)
    col = lax.broadcasted_iota(jnp.int32, (rank, rank), 1)
    work = jnp.concatenate([gram, jnp.where(row == col, 1.0, 0.0)], axis=1)
    wide = work.shape[1]
    row = lax.broadcasted_iota(jnp.int32, (rank, wide), 0)
    scale = jnp.ones((rank, wide), F32)
    for start in range(0, rank, group):
        cols = [
            jnp.broadcast_to(work[:, start + j : start + j + 1], (rank, wide))
            for j in range(group)
        ]
        for j in range(group):
            k = start + j
            pivot = jnp.broadcast_to(cols[j][k : k + 1, :], (rank, wide))
            factor = jnp.where(row > k, cols[j] / pivot, 0.0)
            scale = jnp.where(row == k, lax.rsqrt(pivot), scale)
            work = work - factor * work[k : k + 1, :]
            for i in range(j + 1, group):
                cols[i] = cols[i] - factor * cols[i][k : k + 1, :]
    return (work * scale)[:, rank:]


def final_kernel(
    place_ref, near_ref, far_ref, left_ref, near_matrix_ref, far_matrix_ref, warm_ref, q_ref, update_ref, error_ref, *, groups
):
    width = near_ref.shape[1]
    near = pl.ds(pl.multiple_of(place_ref[1] * width, width), width)
    far = pl.ds(pl.multiple_of((1 - place_ref[1]) * width, width), width)
    gram = dot_nt(near_ref[...], warm_ref[:, near], HIGHEST) + dot_nt(
        far_ref[...], warm_ref[:, far], HIGHEST
    )
    inverse = inverse_factor(gram)
    ortho = dot_nn(inverse, left_ref[...], HIGHEST)
    for columns, right_ref, matrix_ref in (
        (near, near_ref, near_matrix_ref),
        (far, far_ref, far_matrix_ref),
    ):
        new_q = dot_nn(inverse, right_ref[...], HIGHEST) / groups
        update = dot_tn(ortho, new_q, HIGHEST)
        q_ref[:, columns] = new_q
        update_ref[:, columns] = update
        error_ref[:, columns] = matrix_ref[...] - update


def stage_order(bits, swapped):
    order = list(range(bits))
    if swapped and bits > 1:
        order[0], order[1] = 1, 0
    return order


def exchange(x, axes, size, mask):
    return lax.ppermute(x, axes, [(i, i ^ mask) for i in range(size)])


def body(
    node_state,
    edge_state,
    senders,
    receivers,
    send_index,
    cotangent,
    w_edge,
    w_node,
    error_memory,
    warm_q,
):
    node_block = node_state[0]
    edge_block = edge_state[0]
    nodes, features = node_block.shape
    edges = edge_block.shape[0]
    partitions = lax.axis_size("graph")
    replicas = lax.axis_size("dp")
    rank = warm_q.shape[1]
    warm = warm_q.T
    tile = 512
    params = functools.partial(pltpu.CompilerParams, vmem_limit_bytes=24 * MIB)

    vmem = pl.BlockSpec(memory_space=pltpu.VMEM)
    hbm = pl.BlockSpec(memory_space=pltpu.HBM)
    outgoing = pl.pallas_call(
        pick_kernel,
        in_specs=[hbm] * 2,
        out_specs=vmem,
        out_shape=jax.ShapeDtypeStruct((send_index.shape[2], features), BF16),
        scratch_shapes=[
            pltpu.VMEM((1, send_index.shape[2]), jnp.int32),
            pltpu.VMEM(node_block.shape, BF16),
            pltpu.SemaphoreType.DMA((2,)),
        ],
        compiler_params=pltpu.CompilerParams(vmem_limit_bytes=60 * MIB),
    )(send_index[0], node_block)
    incoming = lax.all_to_all(
        outgoing.reshape(partitions, -1, features), "graph", split_axis=0, concat_axis=0, tiled=True
    ).reshape(-1, features)

    reach = nodes + incoming.shape[0]
    rows = w_node.shape[0] // partitions
    width = features // 2
    place = jnp.stack([lax.axis_index("graph"), lax.axis_index("dp") % 2]).astype(jnp.int32)
    smem = pl.BlockSpec(memory_space=pltpu.SMEM)
    piece = (partitions // 2, rows, width)
    new_block, near_send, near_keep, far_send, far_keep = pl.pallas_call(
        functools.partial(layer_kernel, tile=tile),
        in_specs=[smem] + [vmem] * 3 + [hbm] * 5,
        out_specs=[vmem] * 5,
        out_shape=[
            jax.ShapeDtypeStruct(node_block.shape, BF16),
            jax.ShapeDtypeStruct(piece, BF16),
            jax.ShapeDtypeStruct(piece, F32),
            jax.ShapeDtypeStruct(piece, BF16),
            jax.ShapeDtypeStruct(piece, F32),
        ],
        scratch_shapes=[
            pltpu.VMEM(w_node.shape, F32),
            pltpu.VMEM((edges, features), BF16),
            pltpu.VMEM((reach, features), BF16),
            pltpu.VMEM(w_edge.shape, BF16),
            pltpu.VMEM((features + reach + nodes, features), BF16),
            pltpu.VMEM((nodes, features), F32),
            pltpu.VMEM((nodes, features), BF16),
            pltpu.VMEM((nodes, w_node.shape[0]), BF16),
            pltpu.VMEM(w_node.shape, BF16),
            pltpu.SemaphoreType.DMA((6,)),
            pltpu.SemaphoreType.DMA((edges // tile,)),
        ],
        compiler_params=pltpu.CompilerParams(vmem_limit_bytes=60 * MIB),
    )(
        place,
        senders,
        receivers,
        incoming,
        edge_block,
        node_block,
        cotangent[0],
        w_edge,
        w_node,
    )

    bits = partitions.bit_length() - 1
    near_order, far_order = stage_order(bits, False), stage_order(bits, True)

    def swap(x, bit):
        return exchange(x, "graph", partitions, 1 << bit)

    def halve(keep, got):
        total = keep + got.astype(F32)
        count = total.shape[-3] // 2
        return total[..., :count, :, :], total[..., count:, :, :].astype(BF16)

    near_got = swap(near_send, near_order[0])
    far_got = swap(far_send, far_order[0])
    near_keep, near_send = halve(near_keep, near_got)
    far_keep, far_send = halve(far_keep, far_got)
    near_got = swap(near_send, near_order[1])
    far_got = swap(far_send, far_order[1])
    keep = jnp.stack([near_keep, far_keep])
    got = jnp.stack([near_got, far_got])
    for bit in near_order[2:]:
        keep, send = halve(keep, got)
        got = swap(send, bit)

    near_matrix, far_matrix = pl.pallas_call(
        matrix_kernel,
        in_specs=[smem] + [vmem] * 3,
        out_shape=[jax.ShapeDtypeStruct((rows, width), F32)] * 2,
        compiler_params=params(),
    )(place, keep, got, error_memory[0])
    mean = near_matrix + exchange(far_matrix, "dp", replicas, 1)
    mask = 2
    while 2 * mask < replicas:
        mean = mean + exchange(mean, "dp", replicas, mask)
        mask *= 2
    got = exchange(mean, "dp", replicas, mask)
    total, left = pl.pallas_call(
        left_kernel,
        in_specs=[smem] + [vmem] * 3,
        out_shape=[
            jax.ShapeDtypeStruct((rows, width), F32),
            jax.ShapeDtypeStruct((rank, rows), F32),
        ],
        compiler_params=params(),
    )(place, mean, got, warm)
    other = exchange(left, "dp", replicas, 1)
    left, right = pl.pallas_call(
        right_kernel,
        out_shape=[
            jax.ShapeDtypeStruct((rank, rows), F32),
            jax.ShapeDtypeStruct((rank, width), F32),
        ],
        compiler_params=params(),
    )(left, other, total)
    for bit in range(bits):
        right = right + swap(right, bit)
    far_right = exchange(right, "dp", replicas, 1)

    new_q, update, new_error = pl.pallas_call(
        functools.partial(final_kernel, groups=replicas),
        in_specs=[smem] + [vmem] * 6,
        out_shape=[
            jax.ShapeDtypeStruct((rank, features), F32),
            jax.ShapeDtypeStruct((rows, features), F32),
            jax.ShapeDtypeStruct((rows, features), F32),
        ],
        compiler_params=params(),
    )(place, right, far_right, left, near_matrix, far_matrix, warm)
    return (new_block[None], update, new_error[None], new_q.T)


def solution(mesh):
    return jax.shard_map(
        body,
        mesh=mesh,
        in_specs=(
            P("dp", "graph", None),
            P("dp", "graph", None),
            P("dp", "graph"),
            P("dp", "graph"),
            P("dp", "graph", None),
            P("dp", "graph", None),
            P(),
            P(),
            P("dp", "graph", None),
            P(),
        ),
        out_specs=(P("dp", "graph", None), P("graph", None), P("dp", "graph", None), P()),
        check_vma=False,
    )
```

time: 98.3 us -> 80.5 us (0.82)
  blocking collectives: 31.2 us -> 0 us
  waiting for transfers between devices: 19 us -> 42 us
  local copies, waits for them, and re-layouts: 13.9 us -> 0.75 us
  other arithmetic: 0.1 us -> 1.86 us
  Pallas kernels: 18.4 us -> 19.6 us
  starting transfers between devices: 14.3 us -> 15.3 us
    all_to_all x1 -> x0, blocking collectives: 31.2 us -> none  [body(): lax.all_to_all(gradient.reshape(partitions, rows, features), 'graph', spl...]
    ppermute x8 -> x12, waiting for transfers between devices: 19 us -> 35.7 us  [exchange(): return lax.ppermute(x, axes, [(i, i ^ mask) for i in range(size)])]
    unnamed x36 -> x10, local copies, waits for them, and re-layouts: 13.9 us -> 0.65 us
    all_to_all x1, waiting for transfers between devices: 0.01 us -> 6.3 us  [body(): lax.all_to_all(outgoing.reshape(partitions, -1, features), 'graph', split...]
    add x7, other arithmetic: 0.07 us -> 1.25 us  [the longest x3 1.21 us: halve(): total = keep + got.astype(F32)]
    pallas_call x6, Pallas kernels: 18.4 us -> 19.6 us  [the longest x1 11.9 us: body(): pl.pallas_call(functools.partial(layer_kernel, tile=tile), in_specs=[smem...]
    ppermute x8 -> x12, starting transfers between devices: 7 us -> 7.97 us  [exchange(): return lax.ppermute(x, axes, [(i, i ^ mask) for i in range(size)])]
  transfers between devices with their start and end apart: 9 -> 13, of which waited for: 8 -> 12; matrix products, arithmetic and copies ran while one was open for 0% -> 2% of each run, Pallas kernels for 6% -> 0%
where the time goes in v2:
time: 80.5 us; the launch traced here: 80.2 us
  waiting for transfers between devices  42 us (52%)
  Pallas kernels  19.6 us (24%)
  starting transfers between devices  15.3 us (19%)
  other arithmetic  1.86 us (2%)
  between operations  0.81 us (1%)
    ppermute x12, waiting for transfers between devices, exchange(): return lax.ppermute(x, axes, [(i, i ^ mask) for i in range(size)])  35.7 us
    pallas_call x1, Pallas kernels, body(): pl.pallas_call(functools.partial(layer_kernel, tile=tile), in_specs=[smem...  11.9 us
    ppermute x12, starting transfers between devices, exchange(): return lax.ppermute(x, axes, [(i, i ^ mask) for i in range(size)])  7.97 us
    all_to_all x1, starting transfers between devices, body(): lax.all_to_all(outgoing.reshape(partitions, -1, features), 'graph', split...  7.29 us
    all_to_all x1, waiting for transfers between devices, body(): lax.all_to_all(outgoing.reshape(partitions, -1, features), 'graph', split...  6.3 us
    pallas_call x1, Pallas kernels, body(): pl.pallas_call(functools.partial(final_kernel, groups=replicas), in_specs...  4.21 us
    pallas_call x1, Pallas kernels, body(): pl.pallas_call(pick_kernel, in_specs=[hbm] * 2, out_specs=vmem, out_shape...  1.94 us
  transfers between devices with their start and end apart: 13, of which 12 were waited for; matrix products, arithmetic and copies ran while one was open for 2% of the time, Pallas kernels for 0%

profile of v2, /device:TPU:0, one launch (start us, length us, event | category | flops | bytes accessed | tf_op | source)
XLA Modules:
  0.0 80.2 jit_solution(14167657952002612751)
XLA Ops:
  0.6 1.9 %shard_map.129 = bf16[64,512]{1,0:T(8,128)(2,1)} custom-call(s32[1,64]{1,0:T(1,128)} %bitcast.30, bf16[512,512]{1,0:T(8,128)(2,1)} %bitcast.23), custom_call_target="tpu_custom_call" | custom-call | tf_op jit(solution)/shard_map/pallas_call | solution.py:299
  2.6 7.3 %all-to-all-start = ((bf16[8,8,512]{2,1,0:T(8,128)(2,1)}), bf16[8,8,512]{2,1,0:T(8,128)(2,1)S(1)}, u32[]{:S(2)}, u32[]{:S(2)}) async-start(bf16[8,8,512]{2,1,0:T(8,128)(2,1)} %bitcast.27), calls=%async_computation | async-start | bytes 131072 | tf_op jit(solution)/shard_map/all_to_all | solution.py:311
  9.9 0.6 pad_add_fusion.place_ref
  10.5 6.3 %all-to-all-done = bf16[8,8,512]{2,1,0:T(8,128)(2,1)S(1)} async-done(((bf16[8,8,512]{2,1,0:T(8,128)(2,1)}), bf16[8,8,512]{2,1,0:T(8,128)(2,1)S(1)}, u32[]{:S(2)}, u32[]{:S(2)}) %all-to-all-start) | async-done | bytes 65568 | tf_op jit(solution)/shard_map/all_to_all | solution.py:311
  16.8 0.0 copy-start.4
  16.8 0.6 copy-done.4
  17.4 11.9 %shard_map.130 = (bf16[512,512]{1,0:T(8,128)(2,1)}, bf16[4,128,256]{2,1,0:T(8,128)(2,1)}, f32[4,128,256]{2,1,0:T(8,128)}, bf16[4,128,256]{2,1,0:T(8,128)(2,1)}, f32[4,128,256]{2,1,0:T(8,128)}) custom-call(s32[2]{0:T(128)} %pad_add_fusion.place_ref, s32[1,2048]{1,0:T(1,128)} %send_ref.1, s32[1,2048]{1,0:T(1,128)} %recv_ref.1, bf16[64,512]{1,0:T(8,128)(2,1)} %bitcast.26, ...), custom_call_target="tpu_custom_call" | custom-call | tf_op jit(solution)/shard_map/pallas_call | solution.py:321
  29.3 0.0 copy-start.3
  29.3 0.5 collective-permute-start
  29.7 0.8 %collective-permute-start.1 = (bf16[4,128,256]{2,1,0:T(8,128)(2,1)}, bf16[4,128,256]{2,1,0:T(8,128)(2,1)S(1)}, u32[]{:S(2)}, u32[]{:S(2)}) collective-permute-start(bf16[4,128,256]{2,1,0:T(8,128)(2,1)} %get-tuple-element.22), channel_id=1, source_target_pairs={{0,8},{4,12},{8,0},{12,4},{16,24},{20,28},{24,16},{28,20},{1,9},{5... | collective-permute-start | bytes 786440 | tf_op jit(solution)/shard_map/ppermute | solution.py:271
  30.6 5.6 %collective-permute-done = bf16[4,128,256]{2,1,0:T(8,128)(2,1)S(1)} collective-permute-done((bf16[4,128,256]{2,1,0:T(8,128)(2,1)}, bf16[4,128,256]{2,1,0:T(8,128)(2,1)S(1)}, u32[]{:S(2)}, u32[]{:S(2)}) %collective-permute-start) | collective-permute-done | bytes 262176 | tf_op jit(solution)/shard_map/ppermute | solution.py:271
  36.2 1.1 %convert_add_fusion.1 = f32[4,128,256]{2,1,0:T(8,128)S(1)} fusion(f32[4,128,256]{2,1,0:T(8,128)} %get-tuple-element.19, bf16[4,128,256]{2,1,0:T(8,128)(2,1)S(1)} %collective-permute-done), kind=kLoop, calls=%fused_computation.2 | loop fusion | flops 262144 | bytes 1310720 | tf_op jit(solution)/shard_map/add | solution.py:365
  37.3 0.3 collective-permute-start.2
  37.6 0.0 collective-permute-done.1
  37.7 0.0 copy-done.3
  37.7 0.0 copy-start.1
  37.7 0.0 copy-start.2
  37.7 0.1 convert_add_fusion
  37.8 0.0 copy-start
  37.8 1.3 %collective-permute-start.3 = (bf16[2,128,256]{2,1,0:T(8,128)(2,1)S(1)}, bf16[2,128,256]{2,1,0:T(8,128)(2,1)S(1)}, u32[]{:S(2)}, u32[]{:S(2)}) collective-permute-start(bf16[2,128,256]{2,1,0:T(8,128)(2,1)S(1)} %slice.39), channel_id=1, source_target_pairs={{0,4},{4,0},{8,12},{12,8},{16,20},{20,16},{24,28},{28,24},{1,5},{5... | collective-permute-start | bytes 393224 | tf_op jit(solution)/shard_map/ppermute | solution.py:271
  39.1 3.2 %collective-permute-done.2 = bf16[2,128,256]{2,1,0:T(8,128)(2,1)S(1)} collective-permute-done((bf16[2,128,256]{2,1,0:T(8,128)(2,1)S(1)}, bf16[2,128,256]{2,1,0:T(8,128)(2,1)S(1)}, u32[]{:S(2)}, u32[]{:S(2)}) %collective-permute-start.2) | collective-permute-done | bytes 131104 | tf_op jit(solution)/shard_map/ppermute | solution.py:271
  42.3 0.5 collective-permute-done.3
  42.8 0.1 maximum_add_fusion
  42.9 1.0 %collective-permute-start.4 = (bf16[2,1,128,256]{3,2,1,0:T(8,128)(2,1)S(1)}, bf16[2,1,128,256]{3,2,1,0:T(8,128)(2,1)S(1)}, u32[]{:S(2)}, u32[]{:S(2)}) collective-permute-start(bf16[2,1,128,256]{3,2,1,0:T(8,128)(2,1)S(1)} %slice.38), channel_id=1, source_target_pairs={{0,16},{4,20},{8,24},{12,28},{16,0},{20,4},{24,8},{28,12},{1,17},{... | collective-permute-start | bytes 393224 | tf_op jit(solution)/shard_map/ppermute | solution.py:271
  43.9 6.3 %collective-permute-done.4.got_ref = bf16[2,1,128,256]{3,2,1,0:T(8,128)(2,1)S(1)} collective-permute-done((bf16[2,1,128,256]{3,2,1,0:T(8,128)(2,1)S(1)}, bf16[2,1,128,256]{3,2,1,0:T(8,128)(2,1)S(1)}, u32[]{:S(2)}, u32[]{:S(2)}) %collective-permute-start.4) | collective-permute-done | bytes 131104 | tf_op jit(solution)/shard_map/ppermute | solution.py:271
  50.2 0.0 copy-done.1
  50.2 0.0 copy-done.2
  50.2 0.6 shard_map.131
  50.8 0.1 collective-permute-start.5
  50.9 1.3 %collective-permute-done.5 = f32[128,256]{1,0:T(8,128)S(1)} collective-permute-done((f32[128,256]{1,0:T(8,128)S(1)}, f32[128,256]{1,0:T(8,128)S(1)}, u32[]{:S(2)}, u32[]{:S(2)}) %collective-permute-start.5) | collective-permute-done | bytes 131104 | tf_op jit(solution)/shard_map/ppermute | solution.py:271
  52.3 1.6 %collective-permute-start.6 = (f32[128,256]{1,0:T(8,128)S(1)}, f32[128,256]{1,0:T(8,128)S(1)}, u32[]{:S(2)}, u32[]{:S(2)}) collective-permute-start(f32[128,256]{1,0:T(8,128)S(1)} %add.29.mean_ref), channel_id=1, source_target_pairs={{0,2},{1,3},{2,0},{3,1},{4,6},{5,7},{6,4},{7,5},{8,10},{9,11},{10,... | collective-permute-start | bytes 393224 | tf_op jit(solution)/shard_map/ppermute | solution.py:271
  53.9 4.0 %collective-permute-done.6.got_ref = f32[128,256]{1,0:T(8,128)S(1)} collective-permute-done((f32[128,256]{1,0:T(8,128)S(1)}, f32[128,256]{1,0:T(8,128)S(1)}, u32[]{:S(2)}, u32[]{:S(2)}) %collective-permute-start.6) | collective-permute-done | bytes 131104 | tf_op jit(solution)/shard_map/ppermute | solution.py:271
  57.9 0.0 copy-done
  57.9 0.8 shard_map.132
  58.7 0.1 collective-permute-start.7
  58.8 1.2 %collective-permute-done.7.other_ref = f32[64,128]{1,0:T(8,128)S(1)} collective-permute-done((f32[64,128]{1,0:T(8,128)S(1)}, f32[64,128]{1,0:T(8,128)S(1)}, u32[]{:S(2)}, u32[]{:S(2)}) %collective-permute-start.7) | collective-permute-done | bytes 32800 | tf_op jit(solution)/shard_map/ppermute | solution.py:271
  60.0 0.2 shard_map.133
  60.2 1.3 %collective-permute-start.8 = (f32[64,256]{1,0:T(8,128)S(1)}, f32[64,256]{1,0:T(8,128)S(1)}, u32[]{:S(2)}, u32[]{:S(2)}) collective-permute-start(f32[64,256]{1,0:T(8,128)S(1)} %get-tuple-element.27), channel_id=1, source_target_pairs={{0,4},{4,0},{8,12},{12,8},{16,20},{20,16},{24,28},{28,24},{1,5},{5... | collective-permute-start | bytes 196616 | tf_op jit(solution)/shard_map/ppermute | solution.py:271
  61.5 3.0 %collective-permute-done.8 = f32[64,256]{1,0:T(8,128)S(1)} collective-permute-done((f32[64,256]{1,0:T(8,128)S(1)}, f32[64,256]{1,0:T(8,128)S(1)}, u32[]{:S(2)}, u32[]{:S(2)}) %collective-permute-start.8) | collective-permute-done | bytes 65568 | tf_op jit(solution)/shard_map/ppermute | solution.py:271
  64.5 0.5 collective-permute-start.9
  65.0 3.8 %collective-permute-done.9 = f32[64,256]{1,0:T(8,128)S(1)} collective-permute-done((f32[64,256]{1,0:T(8,128)S(1)}, f32[64,256]{1,0:T(8,128)S(1)}, u32[]{:S(2)}, u32[]{:S(2)}) %collective-permute-start.9) | collective-permute-done | bytes 65568 | tf_op jit(solution)/shard_map/ppermute | solution.py:271
  68.9 0.4 collective-permute-start.10
  69.3 5.4 %collective-permute-done.10 = f32[64,256]{1,0:T(8,128)S(1)} collective-permute-done((f32[64,256]{1,0:T(8,128)S(1)}, f32[64,256]{1,0:T(8,128)S(1)}, u32[]{:S(2)}, u32[]{:S(2)}) %collective-permute-start.10) | collective-permute-done | bytes 65568 | tf_op jit(solution)/shard_map/ppermute | solution.py:271
  74.7 0.1 collective-permute-start.11
  74.8 1.2 %collective-permute-done.11.far_ref = f32[64,256]{1,0:T(8,128)S(1)} collective-permute-done((f32[64,256]{1,0:T(8,128)S(1)}, f32[64,256]{1,0:T(8,128)S(1)}, u32[]{:S(2)}, u32[]{:S(2)}) %collective-permute-start.11) | collective-permute-done | bytes 65568 | tf_op jit(solution)/shard_map/ppermute | solution.py:271
  76.0 4.2 %shard_map.134 = (f32[64,512]{1,0:T(8,128)}, f32[128,512]{1,0:T(8,128)}, f32[128,512]{1,0:T(8,128)}) custom-call(s32[2]{0:T(128)S(1)} %copy-done.2, f32[64,256]{1,0:T(8,128)S(1)} %add.32.near_ref, f32[64,256]{1,0:T(8,128)S(1)} %collective-permute-done.11.far_ref, f32[64,128]{1,0:T(8,128)S(1)} %get-tuple-element.28.left_ref, ...), custom_call_target="tpu_custom_call" | custom-call | tf_op jit(solution)/shard_map/pallas_call | solution.py:415
  (10 shorter events, 0.1 us)
Async XLA Ops:
  2.6 14.2 %all-to-all-start = ((bf16[8,8,512]{2,1,0:T(8,128)(2,1)}), bf16[8,8,512]{2,1,0:T(8,128)(2,1)S(1)}, u32[]{:S(2)}, u32[]{:S(2)}) async-start(bf16[8,8,512]{2,1,0:T(8,128)(2,1)} %bitcast.27), calls=%async_computation | async-start | bytes 131072 | tf_op jit(solution)/shard_map/all_to_all | solution.py:311
  16.8 0.6 copy-start.4
  29.3 8.4 %copy-start.3 = (f32[4,128,256]{2,1,0:T(8,128)S(1)}, f32[4,128,256]{2,1,0:T(8,128)}, u32[]{:S(2)}) copy-start(f32[4,128,256]{2,1,0:T(8,128)} %get-tuple-element.21) | copy-start | bytes 1572868
  29.3 6.9 %collective-permute-start = (bf16[4,128,256]{2,1,0:T(8,128)(2,1)}, bf16[4,128,256]{2,1,0:T(8,128)(2,1)S(1)}, u32[]{:S(2)}, u32[]{:S(2)}) collective-permute-start(bf16[4,128,256]{2,1,0:T(8,128)(2,1)} %get-tuple-element.20), channel_id=1, source_target_pairs={{0,4},{4,0},{8,12},{12,8},{16,20},{20,16},{24,28},{28,24},{1,5},{5... | collective-permute-start | bytes 786440 | tf_op jit(solution)/shard_map/ppermute | solution.py:271
  29.7 7.9 %collective-permute-start.1 = (bf16[4,128,256]{2,1,0:T(8,128)(2,1)}, bf16[4,128,256]{2,1,0:T(8,128)(2,1)S(1)}, u32[]{:S(2)}, u32[]{:S(2)}) collective-permute-start(bf16[4,128,256]{2,1,0:T(8,128)(2,1)} %get-tuple-element.22), channel_id=1, source_target_pairs={{0,8},{4,12},{8,0},{12,4},{16,24},{20,28},{24,16},{28,20},{1,9},{5... | collective-permute-start | bytes 786440 | tf_op jit(solution)/shard_map/ppermute | solution.py:271
  37.3 5.0 %collective-permute-start.2 = (bf16[2,128,256]{2,1,0:T(8,128)(2,1)S(1)}, bf16[2,128,256]{2,1,0:T(8,128)(2,1)S(1)}, u32[]{:S(2)}, u32[]{:S(2)}) collective-permute-start(bf16[2,128,256]{2,1,0:T(8,128)(2,1)S(1)} %slice.40), channel_id=1, source_target_pairs={{0,8},{4,12},{8,0},{12,4},{16,24},{20,28},{24,16},{28,20},{1,9},{5... | collective-permute-start | bytes 393224 | tf_op jit(solution)/shard_map/ppermute | solution.py:271
  37.7 12.6 %copy-start.1 = (f32[1,128,512]{2,1,0:T(8,128)S(1)}, f32[1,128,512]{2,1,0:T(8,128)}, u32[]{:S(2)}) copy-start(f32[1,128,512]{2,1,0:T(8,128)} %param.18) | copy-start | bytes 786436
  37.7 12.6 %copy-start.2 = (s32[2]{0:T(128)S(1)}, s32[2]{0:T(128)}, u32[]{:S(2)}) copy-start(s32[2]{0:T(128)} %pad_add_fusion.place_ref) | copy-start | bytes 28
  37.8 20.1 %copy-start = (f32[512,64]{0,1:T(8,128)S(1)}, f32[512,64]{0,1:T(8,128)}, u32[]{:S(2)}) copy-start(f32[512,64]{0,1:T(8,128)} %param.19) | copy-start | bytes 393220
  37.8 5.0 %collective-permute-start.3 = (bf16[2,128,256]{2,1,0:T(8,128)(2,1)S(1)}, bf16[2,128,256]{2,1,0:T(8,128)(2,1)S(1)}, u32[]{:S(2)}, u32[]{:S(2)}) collective-permute-start(bf16[2,128,256]{2,1,0:T(8,128)(2,1)S(1)} %slice.39), channel_id=1, source_target_pairs={{0,4},{4,0},{8,12},{12,8},{16,20},{20,16},{24,28},{28,24},{1,5},{5... | collective-permute-start | bytes 393224 | tf_op jit(solution)/shard_map/ppermute | solution.py:271
  42.9 7.3 %collective-permute-start.4 = (bf16[2,1,128,256]{3,2,1,0:T(8,128)(2,1)S(1)}, bf16[2,1,128,256]{3,2,1,0:T(8,128)(2,1)S(1)}, u32[]{:S(2)}, u32[]{:S(2)}) collective-permute-start(bf16[2,1,128,256]{3,2,1,0:T(8,128)(2,1)S(1)} %slice.38), channel_id=1, source_target_pairs={{0,16},{4,20},{8,24},{12,28},{16,0},{20,4},{24,8},{28,12},{1,17},{... | collective-permute-start | bytes 393224 | tf_op jit(solution)/shard_map/ppermute | solution.py:271
  50.8 1.4 %collective-permute-start.5 = (f32[128,256]{1,0:T(8,128)S(1)}, f32[128,256]{1,0:T(8,128)S(1)}, u32[]{:S(2)}, u32[]{:S(2)}) collective-permute-start(f32[128,256]{1,0:T(8,128)S(1)} %get-tuple-element.24.far_matrix_ref), channel_id=1, source_target_pairs={{0,1},{1,0},{2,3},{3,2},{4,5},{5,4},{6,7},{7,6},{8,9},{9,8},{10,11... | collective-permute-start | bytes 393224 | tf_op jit(solution)/shard_map/ppermute | solution.py:271
  52.3 5.6 %collective-permute-start.6 = (f32[128,256]{1,0:T(8,128)S(1)}, f32[128,256]{1,0:T(8,128)S(1)}, u32[]{:S(2)}, u32[]{:S(2)}) collective-permute-start(f32[128,256]{1,0:T(8,128)S(1)} %add.29.mean_ref), channel_id=1, source_target_pairs={{0,2},{1,3},{2,0},{3,1},{4,6},{5,7},{6,4},{7,5},{8,10},{9,11},{10,... | collective-permute-start | bytes 393224 | tf_op jit(solution)/shard_map/ppermute | solution.py:271
  58.7 1.3 %collective-permute-start.7 = (f32[64,128]{1,0:T(8,128)S(1)}, f32[64,128]{1,0:T(8,128)S(1)}, u32[]{:S(2)}, u32[]{:S(2)}) collective-permute-start(f32[64,128]{1,0:T(8,128)S(1)} %get-tuple-element.25.left_ref), channel_id=1, source_target_pairs={{0,1},{1,0},{2,3},{3,2},{4,5},{5,4},{6,7},{7,6},{8,9},{9,8},{10,11... | collective-permute-start | bytes 98312 | tf_op jit(solution)/shard_map/ppermute | solution.py:271
  60.2 4.3 %collective-permute-start.8 = (f32[64,256]{1,0:T(8,128)S(1)}, f32[64,256]{1,0:T(8,128)S(1)}, u32[]{:S(2)}, u32[]{:S(2)}) collective-permute-start(f32[64,256]{1,0:T(8,128)S(1)} %get-tuple-element.27), channel_id=1, source_target_pairs={{0,4},{4,0},{8,12},{12,8},{16,20},{20,16},{24,28},{28,24},{1,5},{5... | collective-permute-start | bytes 196616 | tf_op jit(solution)/shard_map/ppermute | solution.py:271
  64.5 4.3 %collective-permute-start.9 = (f32[64,256]{1,0:T(8,128)S(1)}, f32[64,256]{1,0:T(8,128)S(1)}, u32[]{:S(2)}, u32[]{:S(2)}) collective-permute-start(f32[64,256]{1,0:T(8,128)S(1)} %add.30), channel_id=1, source_target_pairs={{0,8},{4,12},{8,0},{12,4},{16,24},{20,28},{24,16},{28,20},{1,9},{5... | collective-permute-start | bytes 196616 | tf_op jit(solution)/shard_map/ppermute | solution.py:271
  68.9 5.8 %collective-permute-start.10 = (f32[64,256]{1,0:T(8,128)S(1)}, f32[64,256]{1,0:T(8,128)S(1)}, u32[]{:S(2)}, u32[]{:S(2)}) collective-permute-start(f32[64,256]{1,0:T(8,128)S(1)} %add.31), channel_id=1, source_target_pairs={{0,16},{4,20},{8,24},{12,28},{16,0},{20,4},{24,8},{28,12},{1,17},{... | collective-permute-start | bytes 196616 | tf_op jit(solution)/shard_map/ppermute | solution.py:271
  74.7 1.3 %collective-permute-start.11 = (f32[64,256]{1,0:T(8,128)S(1)}, f32[64,256]{1,0:T(8,128)S(1)}, u32[]{:S(2)}, u32[]{:S(2)}) collective-permute-start(f32[64,256]{1,0:T(8,128)S(1)} %add.32.near_ref), channel_id=1, source_target_pairs={{0,1},{1,0},{2,3},{3,2},{4,5},{5,4},{6,7},{7,6},{8,9},{9,8},{10,11... | collective-permute-start | bytes 196616 | tf_op jit(solution)/shard_map/ppermute | solution.py:271

commit v3 on v2

v3 whole, which is shorter than its diff:
```python
import functools

import jax
import jax.numpy as jnp
from jax import lax
from jax.experimental import pallas as pl
from jax.experimental.pallas import tpu as pltpu
from jax.sharding import PartitionSpec as P

F32 = jnp.float32
BF16 = jnp.bfloat16
HIGHEST = lax.Precision.HIGHEST
MIB = 1 << 20


def dot_nn(a, b, precision=None):
    return lax.dot_general(
        a, b, (((1,), (0,)), ((), ())), precision=precision, preferred_element_type=F32
    )


def dot_nt(a, b, precision=None):
    return lax.dot_general(
        a, b, (((1,), (1,)), ((), ())), precision=precision, preferred_element_type=F32
    )


def dot_tn(a, b, precision=None):
    return lax.dot_general(
        a, b, (((0,), (0,)), ((), ())), precision=precision, preferred_element_type=F32
    )


def sigmoid(v):
    return 0.5 * jnp.tanh(0.5 * v) + 0.5


def columns_of(row):
    return jnp.broadcast_to(row, (128, row.shape[1])).T


def hits(a, b):
    return jnp.where(a == b, jnp.ones((), BF16), jnp.zeros((), BF16))


def one_hot_rows(cols, first, width):
    cols = cols.astype(jnp.int16)
    lane = lax.broadcasted_iota(jnp.int32, cols.shape, 1)
    parts = []
    for start in range(0, width, 128):
        size = min(128, width - start)
        parts.append(hits(cols, (lane + (first + start)).astype(jnp.int16))[:, :size])
    return parts[0] if len(parts) == 1 else jnp.concatenate(parts, axis=1)


def one_hot_columns(row, height):
    index = lax.broadcasted_iota(jnp.int32, (height, row.shape[1]), 0).astype(jnp.int16)
    return hits(index, jnp.broadcast_to(row, index.shape).astype(jnp.int16))


def pick_kernel(index_hbm, node_hbm, out_ref, index, node, sems):
    copies = [
        pltpu.make_async_copy(index_hbm, index, sems.at[0]),
        pltpu.make_async_copy(node_hbm, node, sems.at[1]),
    ]
    for copy in copies:
        copy.start()
    for copy in copies:
        copy.wait()
    hit = one_hot_columns(index[...], node.shape[0])
    out_ref[...] = dot_tn(hit, node[...]).astype(BF16)


def edge_kernel(
    send_hbm, recv_hbm, edge_hbm, node_hbm, wedge_hbm, pre_hbm, send, recv, edge, node, weight, table, pre, sems, edge_sems, pre_sems, *, tile
):
    nodes, features = node_hbm.shape
    steps = edge_hbm.shape[0] // tile

    def edge_copy(step):
        rows = pl.ds(step * tile, tile)
        return pltpu.make_async_copy(edge_hbm.at[rows, :], edge.at[rows, :], edge_sems.at[step])

    def pre_copy(step):
        rows = pl.ds(step * tile, tile)
        return pltpu.make_async_copy(pre.at[rows, :], pre_hbm.at[rows, :], pre_sems.at[step])

    node_copy = pltpu.make_async_copy(node_hbm, node, sems.at[0])
    weight_copies = [
        pltpu.make_async_copy(
            wedge_hbm.at[pl.ds(part * features, features), :],
            weight.at[pl.ds(part * features, features), :],
            sems.at[1 + part],
        )
        for part in (1, 2, 0)
    ]
    index_copies = [
        pltpu.make_async_copy(send_hbm, send, sems.at[4]),
        pltpu.make_async_copy(recv_hbm, recv, sems.at[5]),
    ]
    node_copy.start()
    for copy in weight_copies + index_copies:
        copy.start()
    for step in range(steps):
        edge_copy(step).start()
    node_copy.wait()
    weight_copies[0].wait()
    own = dot_nn(node[...], weight[features : 2 * features, :])
    table[features : features + nodes, :] = (0.5 * own).astype(BF16)
    weight_copies[1].wait()
    into = dot_nn(node[...], weight[2 * features :, :])
    table[features + nodes :, :] = (0.5 * into).astype(BF16)
    weight_copies[2].wait()
    table[0:features, :] = weight[0:features, :] * 0.5
    for copy in index_copies:
        copy.wait()
    for step in range(steps):
        rows = pl.ds(step * tile, tile)
        edge_copy(step).wait()
        left = jnp.concatenate(
            [
                edge[rows, :],
                one_hot_rows(columns_of(send[:, rows]), 0, nodes),
                one_hot_rows(columns_of(recv[:, rows]), 0, nodes),
            ],
            axis=1,
        )
        pre[rows, :] = dot_nn(left, table[...]).astype(pre.dtype)
        pre_copy(step).start()
    for step in range(steps):
        pre_copy(step).wait()


def node_kernel(
    send_ref,
    recv_ref,
    halo_ref,
    node_ref,
    cot_ref,
    wnode_ref,
    pre_hbm,
    edge_hbm,
    wedge_hbm,
    new_ref,
    near_send_ref,
    near_keep_ref,
    far_send_ref,
    far_keep_ref,
    pre,
    edge,
    weight,
    table,
    total,
    gathered,
    delta,
    grad,
    sems,
    edge_sems,
    pre_sems,
    *,
    tile,
):
    nodes, features = node_ref.shape
    steps = edge_hbm.shape[0] // tile

    def edge_copy(step):
        rows = pl.ds(step * tile, tile)
        return pltpu.make_async_copy(edge_hbm.at[rows, :], edge.at[rows, :], edge_sems.at[step])

    def pre_copy(step):
        rows = pl.ds(step * tile, tile)
        return pltpu.make_async_copy(pre_hbm.at[rows, :], pre.at[rows, :], pre_sems.at[step])

    weight_copy = pltpu.make_async_copy(
        wedge_hbm.at[pl.ds(features, features), :], weight, sems.at[0]
    )
    weight_copy.start()
    for step in range(steps):
        pre_copy(step).start()
        edge_copy(step).start()
    weight_copy.wait()
    table[...] = (0.5 * dot_nn(halo_ref[...], weight[...])).astype(BF16)
    for step in range(steps):
        rows = pl.ds(step * tile, tile)
        hot = one_hot_rows(columns_of(send_ref[:, rows]), nodes, halo_ref.shape[0])
        incidence = one_hot_columns(recv_ref[:, rows], nodes)
        pre_copy(step).wait()
        edge_copy(step).wait()
        half = pre[rows, :].astype(F32) + dot_nn(hot, table[...])
        edge_new = (edge[rows, :].astype(F32) + (half + half * jnp.tanh(half))).astype(BF16)
        part = dot_nn(incidence, edge_new)
        if step == 0:
            total[...] = part
        else:
            total[...] += part

    gathered[...] = total[...].astype(BF16)
    block = 128
    for step in range(nodes // block):
        rows = pl.ds(step * block, block)
        node = node_ref[rows, :]
        joined = jnp.concatenate([node, gathered[rows, :]], axis=1)
        half = 0.5 * dot_nn(joined, wnode_ref[...])
        turn = jnp.tanh(half)
        new_ref[rows, :] = (node.astype(F32) + (half + half * turn)).astype(BF16)
        slope = (0.5 + 0.5 * turn) * (1.0 + half * (1.0 - turn))
        delta[rows, :] = (cot_ref[rows, :].astype(F32) * slope).astype(BF16)
    grad[0:features, :] = dot_tn(node_ref[...], delta[...])
    grad[features:, :] = dot_tn(gathered[...], delta[...])
    me = lax.axis_index("graph")
    side = lax.axis_index("dp") % 2
    parts, size, width = near_keep_ref.shape
    bits = (2 * parts).bit_length() - 1
    for refs, order, turn in (
        ((near_keep_ref, near_send_ref), stage_order(bits, False), side),
        ((far_keep_ref, far_send_ref), stage_order(bits, True), 1 - side),
    ):
        column = pl.multiple_of(turn * width, width)
        for slot in range(2 * parts):
            offset = 0
            for stage, bit in enumerate(order):
                offset |= ((slot >> (bits - 1 - stage)) & 1) << bit
            row = pl.multiple_of((me ^ offset) * size, size)
            block = grad[pl.ds(row, size), pl.ds(column, width)]
            ref = refs[slot // parts]
            ref[slot % parts] = block.astype(ref.dtype)


def matrix_kernel(keep_ref, got_ref, error_ref, near_ref, far_ref):
    width = near_ref.shape[1]
    side = lax.axis_index("dp") % 2
    for half, (out_ref, turn) in enumerate(((near_ref, side), (far_ref, 1 - side))):
        column = pl.multiple_of(turn * width, width)
        out_ref[...] = (
            keep_ref[half, 0] + got_ref[half, 0].astype(F32) + error_ref[:, pl.ds(column, width)]
        )


def left_kernel(mean_ref, got_ref, warm_ref, sum_ref, left_ref):
    width = mean_ref.shape[1]
    total = mean_ref[...].astype(F32) + got_ref[...].astype(F32)
    sum_ref[...] = total
    column = pl.multiple_of((lax.axis_index("dp") % 2) * width, width)
    left_ref[...] = dot_nt(warm_ref[:, pl.ds(column, width)], total, HIGHEST)


def right_kernel(left_ref, other_ref, sum_ref, full_ref, right_ref):
    left = left_ref[...] + other_ref[...]
    full_ref[...] = left
    right_ref[...] = dot_nn(left, sum_ref[...], HIGHEST)


def inverse_factor(gram, group=8):
    rank = gram.shape[0]
    row = lax.broadcasted_iota(jnp.int32, (rank, rank), 0)
    col = lax.broadcasted_iota(jnp.int32, (rank, rank), 1)
    joined = jnp.concatenate([gram, jnp.where(row == col, 1.0, 0.0)], axis=1)
    wide = joined.shape[1]
    row = lax.broadcasted_iota(jnp.int32, (group, wide), 0)
    work = [joined[start : start + group] for start in range(0, rank, group)]
    for g in range(rank // group):
        cols = [
            {
                b: jnp.broadcast_to(work[b][:, k : k + 1], (group, wide))
                for b in range(g, rank // group)
            }
            for k in range(g * group, (g + 1) * group)
        ]
        scale = jnp.ones((group, wide), F32)
        for j in range(group):
            pivot = cols[j][g][j : j + 1]
            scale = jnp.where(row == j, lax.rsqrt(pivot), scale)
            inverse = 1.0 / pivot
            source = work[g][j : j + 1]
            sources = [cols[i][g][j : j + 1] for i in range(j + 1, group)]
            for b in range(g, rank // group):
                if b == g and j == group - 1:
                    continue
                factor = cols[j][b] * inverse
                if b == g:
                    factor = jnp.where(row > j, factor, 0.0)
                work[b] = work[b] - factor * source
                for i in range(j + 1, group):
                    cols[i][b] = cols[i][b] - factor * sources[i - j - 1]
        work[g] = work[g] * scale
    return jnp.concatenate(work, axis=0)[:, rank:]


def split3(a):
    high = a.astype(BF16)
    return high, (a - high.astype(F32)).astype(BF16)


def dot3_nn(a, b):
    a_high, a_low = split3(a)
    b_high, b_low = split3(b)
    return dot_nn(
        jnp.concatenate([a_high, a_high, a_low], axis=1),
        jnp.concatenate([b_high, b_low, b_high], axis=0),
    )


def dot3_tn(a, b):
    a_high, a_low = split3(a)
    b_high, b_low = split3(b)
    return dot_tn(
        jnp.concatenate([a_high, a_high, a_low], axis=0),
        jnp.concatenate([b_high, b_low, b_high], axis=0),
    )


def final_kernel(
    near_ref,
    far_ref,
    left_ref,
    near_matrix_ref,
    far_matrix_ref,
    warm_ref,
    q_hbm,
    update_hbm,
    error_hbm,
    q_ref,
    update_ref,
    error_ref,
    sems,
    *,
    groups,
):
    width = near_ref.shape[1]
    side = lax.axis_index("dp") % 2
    near = pl.ds(pl.multiple_of(side * width, width), width)
    far = pl.ds(pl.multiple_of((1 - side) * width, width), width)
    gram = dot_nt(near_ref[...], warm_ref[:, near], HIGHEST) + dot_nt(
        far_ref[...], warm_ref[:, far], HIGHEST
    )
    inverse = inverse_factor(gram)
    ortho = dot3_nn(inverse, left_ref[...])
    copies = []
    for half, (columns, right_ref, matrix_ref) in enumerate(
        ((near, near_ref, near_matrix_ref), (far, far_ref, far_matrix_ref))
    ):
        new_q = dot3_nn(inverse, right_ref[...]) / groups
        update = dot3_tn(ortho, new_q)
        q_ref[half] = new_q
        update_ref[half] = update
        error_ref[half] = matrix_ref[...] - update
        for part, (source, target) in enumerate(
            ((q_ref, q_hbm), (update_ref, update_hbm), (error_ref, error_hbm))
        ):
            copies.append(
                pltpu.make_async_copy(source.at[half], target.at[:, columns], sems.at[half, part])
            )
            copies[-1].start()
    for copy in copies:
        copy.wait()


def stage_order(bits, swapped):
    order = list(range(bits))
    if swapped and bits > 1:
        order[0], order[1] = 1, 0
    return order


def exchange(x, axes, size, mask):
    return lax.ppermute(x, axes, [(i, i ^ mask) for i in range(size)])


def body(
    node_state,
    edge_state,
    senders,
    receivers,
    send_index,
    cotangent,
    w_edge,
    w_node,
    error_memory,
    warm_q,
):
    node_block = node_state[0]
    edge_block = edge_state[0]
    nodes, features = node_block.shape
    edges = edge_block.shape[0]
    partitions = lax.axis_size("graph")
    replicas = lax.axis_size("dp")
    rank = warm_q.shape[1]
    warm = warm_q.T
    tile = edges // 2
    params = functools.partial(pltpu.CompilerParams, vmem_limit_bytes=24 * MIB)

    vmem = pl.BlockSpec(memory_space=pltpu.VMEM)
    hbm = pl.BlockSpec(memory_space=pltpu.HBM)
    outgoing = pl.pallas_call(
        pick_kernel,
        in_specs=[hbm] * 2,
        out_specs=vmem,
        out_shape=jax.ShapeDtypeStruct((send_index.shape[2], features), BF16),
        scratch_shapes=[
            pltpu.VMEM((1, send_index.shape[2]), jnp.int32),
            pltpu.VMEM(node_block.shape, BF16),
            pltpu.SemaphoreType.DMA((2,)),
        ],
        compiler_params=pltpu.CompilerParams(vmem_limit_bytes=60 * MIB),
    )(send_index[0], node_block)
    incoming = lax.all_to_all(
        outgoing.reshape(partitions, -1, features), "graph", split_axis=0, concat_axis=0, tiled=True
    ).reshape(-1, features)

    steps = edges // tile
    pre_type = F32
    edge_pre = pl.pallas_call(
        functools.partial(edge_kernel, tile=tile),
        in_specs=[hbm] * 5,
        out_specs=hbm,
        out_shape=jax.ShapeDtypeStruct((edges, features), pre_type),
        scratch_shapes=[
            pltpu.VMEM(senders.shape, jnp.int32),
            pltpu.VMEM(receivers.shape, jnp.int32),
            pltpu.VMEM((edges, features), BF16),
            pltpu.VMEM((nodes, features), BF16),
            pltpu.VMEM(w_edge.shape, BF16),
            pltpu.VMEM((features + 2 * nodes, features), BF16),
            pltpu.VMEM((edges, features), pre_type),
            pltpu.SemaphoreType.DMA((6,)),
            pltpu.SemaphoreType.DMA((steps,)),
            pltpu.SemaphoreType.DMA((steps,)),
        ],
        compiler_params=pltpu.CompilerParams(vmem_limit_bytes=60 * MIB),
    )(senders, receivers, edge_block, node_block, w_edge)
    rows = w_node.shape[0] // partitions
    width = features // 2
    piece = (partitions // 2, rows, width)
    new_block, near_send, near_keep, far_send, far_keep = pl.pallas_call(
        functools.partial(node_kernel, tile=tile),
        in_specs=[vmem] * 6 + [hbm] * 3,
        out_specs=[vmem] * 5,
        out_shape=[
            jax.ShapeDtypeStruct(node_block.shape, BF16),
            jax.ShapeDtypeStruct(piece, BF16),
            jax.ShapeDtypeStruct(piece, F32),
            jax.ShapeDtypeStruct(piece, BF16),
            jax.ShapeDtypeStruct(piece, F32),
        ],
        scratch_shapes=[
            pltpu.VMEM((edges, features), pre_type),
            pltpu.VMEM((edges, features), BF16),
            pltpu.VMEM((features, features), BF16),
            pltpu.VMEM(incoming.shape, BF16),
            pltpu.VMEM((nodes, features), F32),
            pltpu.VMEM((nodes, features), BF16),
            pltpu.VMEM((nodes, features), BF16),
            pltpu.VMEM(w_node.shape, F32),
            pltpu.SemaphoreType.DMA((1,)),
            pltpu.SemaphoreType.DMA((steps,)),
            pltpu.SemaphoreType.DMA((steps,)),
        ],
        compiler_params=pltpu.CompilerParams(vmem_limit_bytes=50 * MIB),
    )(
        senders,
        receivers,
        incoming,
        node_block,
        cotangent[0],
        w_node,
        edge_pre,
        edge_block,
        w_edge,
    )

    bits = partitions.bit_length() - 1
    near_order, far_order = stage_order(bits, False), stage_order(bits, True)

    def swap(x, bit):
        return exchange(x, "graph", partitions, 1 << bit)

    def halve(keep, got):
        total = keep + got.astype(F32)
        count = total.shape[-3] // 2
        return total[..., :count, :, :], total[..., count:, :, :].astype(BF16)

    near_got = swap(near_send, near_order[0])
    far_got = swap(far_send, far_order[0])
    near_keep, near_send = halve(near_keep, near_got)
    far_keep, far_send = halve(far_keep, far_got)
    near_got = swap(near_send, near_order[1])
    far_got = swap(far_send, far_order[1])
    keep = jnp.stack([near_keep, far_keep])
    got = jnp.stack([near_got, far_got])
    for bit in near_order[2:]:
        keep, send = halve(keep, got)
        got = swap(send, bit)

    near_matrix, far_matrix = pl.pallas_call(
        matrix_kernel,
        out_shape=[jax.ShapeDtypeStruct((rows, width), F32)] * 2,
        compiler_params=params(),
    )(keep, got, error_memory[0])
    mean = near_matrix + exchange(far_matrix, "dp", replicas, 1)
    mask = 2
    while 2 * mask < replicas:
        mean = mean + exchange(mean, "dp", replicas, mask)
        mask *= 2
    mean = mean.astype(BF16)
    got = exchange(mean, "dp", replicas, mask)
    total, left = pl.pallas_call(
        left_kernel,
        out_shape=[
            jax.ShapeDtypeStruct((rows, width), F32),
            jax.ShapeDtypeStruct((rank, rows), F32),
        ],
        compiler_params=params(),
    )(mean, got, warm)
    other = exchange(left, "dp", replicas, 1)
    left, right = pl.pallas_call(
        right_kernel,
        out_shape=[
            jax.ShapeDtypeStruct((rank, rows), F32),
            jax.ShapeDtypeStruct((rank, width), F32),
        ],
        compiler_params=params(),
    )(left, other, total)
    along, across = swap(right, 0), swap(right, 1)
    corner = exchange(right, "graph", partitions, 3)
    right = (right + along) + (across + corner)
    for bit in range(2, bits):
        right = right + swap(right, bit)
    far_right = exchange(right, "dp", replicas, 1)

    new_q, update, new_error = pl.pallas_call(
        functools.partial(final_kernel, groups=replicas),
        in_specs=[vmem] * 6,
        out_specs=[hbm] * 3,
        out_shape=[
            jax.ShapeDtypeStruct((rank, features), F32),
            jax.ShapeDtypeStruct((rows, features), F32),
            jax.ShapeDtypeStruct((rows, features), F32),
        ],
        scratch_shapes=[
            pltpu.VMEM((2, rank, width), F32),
            pltpu.VMEM((2, rows, width), F32),
            pltpu.VMEM((2, rows, width), F32),
            pltpu.SemaphoreType.DMA((2, 3)),
        ],
        compiler_params=params(),
    )(right, far_right, left, near_matrix, far_matrix, warm)
    return (new_block[None], update, new_error[None], new_q.T)


def solution(mesh):
    return jax.shard_map(
        body,
        mesh=mesh,
        in_specs=(
            P("dp", "graph", None),
            P("dp", "graph", None),
            P("dp", "graph"),
            P("dp", "graph"),
            P("dp", "graph", None),
            P("dp", "graph", None),
            P(),
            P(),
            P("dp", "graph", None),
            P(),
        ),
        out_specs=(P("dp", "graph", None), P("graph", None), P("dp", "graph", None), P()),
        check_vma=False,
    )
```

time: 80.5 us -> 71.2 us (0.88)
  waiting for transfers between devices: 42 us -> 27.2 us
  starting transfers between devices: 15.3 us -> 23.1 us
  other arithmetic: 1.86 us -> 0.22 us
    ppermute x12 -> x13, waiting for transfers between devices: 35.7 us -> 27.2 us  [exchange(): return lax.ppermute(x, axes, [(i, i ^ mask) for i in range(size)])]
    ppermute x12 -> x13, starting transfers between devices: 7.97 us -> 15.8 us  [exchange(): return lax.ppermute(x, axes, [(i, i ^ mask) for i in range(size)])]
    all_to_all x1, waiting for transfers between devices: 6.3 us -> 0.01 us  [body(): lax.all_to_all(outgoing.reshape(partitions, -1, features), 'graph', split...]
    add x3, other arithmetic: 1.21 us -> 0.18 us  [halve(): total = keep + got.astype(F32)]
    pallas_call x1, Pallas kernels: 4.21 us -> 3.35 us  [body(): pl.pallas_call(functools.partial(final_kernel, groups=replicas), in_specs...]
    pallas_call x3 -> x4, Pallas kernels: 13.2 us -> 14 us  [the longest x1 7.22 us: body(): pl.pallas_call(functools.partial(edge_kernel, tile=tile), in_specs=[hbm]...]
  transfers between devices with their start and end apart: 13 -> 14, of which waited for: 12 -> 12; matrix products, arithmetic and copies ran while one was open for 2% -> 0% of each run, Pallas kernels for 0% -> 10%
where the time goes in v3:
time: 71.2 us; the launch traced here: 71 us
  waiting for transfers between devices  27.2 us (38%)
  starting transfers between devices  23.1 us (32%)
  Pallas kernels  19.5 us (27%)
  between operations  0.86 us (1%)
    ppermute x13, waiting for transfers between devices, exchange(): return lax.ppermute(x, axes, [(i, i ^ mask) for i in range(size)])  27.2 us
    ppermute x13, starting transfers between devices, exchange(): return lax.ppermute(x, axes, [(i, i ^ mask) for i in range(size)])  15.8 us
    all_to_all x1, starting transfers between devices, body(): lax.all_to_all(outgoing.reshape(partitions, -1, features), 'graph', split...  7.29 us
    pallas_call x1, Pallas kernels, body(): pl.pallas_call(functools.partial(edge_kernel, tile=tile), in_specs=[hbm]...  7.22 us
    pallas_call x1, Pallas kernels, body(): pl.pallas_call(functools.partial(node_kernel, tile=tile), in_specs=[vmem]...  6.53 us
    pallas_call x1, Pallas kernels, body(): pl.pallas_call(functools.partial(final_kernel, groups=replicas), in_specs...  3.35 us
    pallas_call x1, Pallas kernels, body(): pl.pallas_call(pick_kernel, in_specs=[hbm] * 2, out_specs=vmem, out_shape...  1.94 us
  transfers between devices with their start and end apart: 14, of which 12 were waited for; matrix products, arithmetic and copies ran while one was open for 0% of the time, Pallas kernels for 10%

profile of v3, /device:TPU:0, one launch (start us, length us, event | category | flops | bytes accessed | tf_op | source)
XLA Modules:
  0.0 71.0 jit_solution(7455747327882334097)
XLA Ops:
  0.6 1.9 %shard_map.129 = bf16[64,512]{1,0:T(8,128)(2,1)} custom-call(s32[1,64]{1,0:T(1,128)} %bitcast.30, bf16[512,512]{1,0:T(8,128)(2,1)} %bitcast.17), custom_call_target="tpu_custom_call" | custom-call | tf_op jit(solution)/shard_map/pallas_call | solution.py:394
  2.6 7.3 %all-to-all-start = ((bf16[8,8,512]{2,1,0:T(8,128)(2,1)}), bf16[8,8,512]{2,1,0:T(8,128)(2,1)S(1)}, u32[]{:S(2)}, u32[]{:S(2)}) async-start(bf16[8,8,512]{2,1,0:T(8,128)(2,1)} %bitcast.27), calls=%async_computation | async-start | bytes 131072 | tf_op jit(solution)/shard_map/all_to_all | solution.py:406
  9.9 0.0 copy-start.1
  9.9 0.0 copy-start.2
  9.9 0.0 copy-start.5
  9.9 0.0 copy-start.6
  9.9 7.2 %shard_map.130.pre_hbm = f32[2048,512]{1,0:T(8,128)} custom-call(s32[1,2048]{1,0:T(1,128)} %send_ref.1, s32[1,2048]{1,0:T(1,128)} %recv_ref.1, bf16[2048,512]{1,0:T(8,128)(2,1)} %bitcast.25, bf16[512,512]{1,0:T(8,128)(2,1)} %bitcast.18, bf16[1536,512]{1,0:T(8,128)(2,1)} %wedge_hbm.3), custom_call_target="tpu_custom_call" | custom-call | tf_op jit(solution)/shard_map/pallas_call | solution.py:412
  17.1 0.0 all-to-all-done
  17.2 0.0 copy-done
  17.2 0.0 copy-done.1
  17.2 0.0 copy-done.2
  17.2 0.0 copy-done.5
  17.2 0.0 copy-done.6
  17.2 6.5 %shard_map.131 = (bf16[512,512]{1,0:T(8,128)(2,1)}, bf16[4,128,256]{2,1,0:T(8,128)(2,1)S(1)}, f32[4,128,256]{2,1,0:T(8,128)S(1)}, bf16[4,128,256]{2,1,0:T(8,128)(2,1)S(1)}, f32[4,128,256]{2,1,0:T(8,128)S(1)}) custom-call(s32[1,2048]{1,0:T(1,128)S(1)} %copy-done.5, s32[1,2048]{1,0:T(1,128)S(1)} %copy-done.6, bf16[64,512]{1,0:T(8,128)(2,1)S(1)} %bitcast.23, ...), custom_call_target="tpu_custom_call" | custom-call | tf_op jit(solution)/shard_map/pallas_call | solution.py:434
  23.7 2.1 %collective-permute-start = (bf16[4,128,256]{2,1,0:T(8,128)(2,1)S(1)}, bf16[4,128,256]{2,1,0:T(8,128)(2,1)S(1)}, u32[]{:S(2)}, u32[]{:S(2)}) collective-permute-start(bf16[4,128,256]{2,1,0:T(8,128)(2,1)S(1)} %get-tuple-element.20), channel_id=1, source_target_pairs={{0,4},{4,0},{8,12},{12,8},{16,20},{20,16},{24,28},{28,24},{1,5},{5... | collective-permute-start | bytes 786440 | tf_op jit(solution)/shard_map/ppermute | solution.py:366
  25.8 1.5 %collective-permute-start.1 = (bf16[4,128,256]{2,1,0:T(8,128)(2,1)S(1)}, bf16[4,128,256]{2,1,0:T(8,128)(2,1)S(1)}, u32[]{:S(2)}, u32[]{:S(2)}) collective-permute-start(bf16[4,128,256]{2,1,0:T(8,128)(2,1)S(1)} %get-tuple-element.22), channel_id=1, source_target_pairs={{0,8},{4,12},{8,0},{12,4},{16,24},{20,28},{24,16},{28,20},{1,9},{5... | collective-permute-start | bytes 786440 | tf_op jit(solution)/shard_map/ppermute | solution.py:366
  27.3 4.3 %collective-permute-done = bf16[4,128,256]{2,1,0:T(8,128)(2,1)S(1)} collective-permute-done((bf16[4,128,256]{2,1,0:T(8,128)(2,1)S(1)}, bf16[4,128,256]{2,1,0:T(8,128)(2,1)S(1)}, u32[]{:S(2)}, u32[]{:S(2)}) %collective-permute-start) | collective-permute-done | bytes 262176 | tf_op jit(solution)/shard_map/ppermute | solution.py:366
  31.6 0.1 convert_add_fusion.1
  31.7 1.8 %collective-permute-start.2 = (bf16[2,128,256]{2,1,0:T(8,128)(2,1)S(1)}, bf16[2,128,256]{2,1,0:T(8,128)(2,1)S(1)}, u32[]{:S(2)}, u32[]{:S(2)}) collective-permute-start(bf16[2,128,256]{2,1,0:T(8,128)(2,1)S(1)} %slice.40), channel_id=1, source_target_pairs={{0,8},{4,12},{8,0},{12,4},{16,24},{20,28},{24,16},{28,20},{1,9},{5... | collective-permute-start | bytes 393224 | tf_op jit(solution)/shard_map/ppermute | solution.py:366
  33.5 0.0 collective-permute-done.1
  33.5 0.0 copy-start.4
  33.5 0.1 convert_add_fusion
  33.6 0.0 copy-start.3
  33.6 1.5 %collective-permute-start.3 = (bf16[2,128,256]{2,1,0:T(8,128)(2,1)S(1)}, bf16[2,128,256]{2,1,0:T(8,128)(2,1)S(1)}, u32[]{:S(2)}, u32[]{:S(2)}) collective-permute-start(bf16[2,128,256]{2,1,0:T(8,128)(2,1)S(1)} %slice.39), channel_id=1, source_target_pairs={{0,4},{4,0},{8,12},{12,8},{16,20},{20,16},{24,28},{28,24},{1,5},{5... | collective-permute-start | bytes 393224 | tf_op jit(solution)/shard_map/ppermute | solution.py:366
  35.2 1.5 %collective-permute-done.2 = bf16[2,128,256]{2,1,0:T(8,128)(2,1)S(1)} collective-permute-done((bf16[2,128,256]{2,1,0:T(8,128)(2,1)S(1)}, bf16[2,128,256]{2,1,0:T(8,128)(2,1)S(1)}, u32[]{:S(2)}, u32[]{:S(2)}) %collective-permute-start.2) | collective-permute-done | bytes 131104 | tf_op jit(solution)/shard_map/ppermute | solution.py:366
  36.7 1.9 %collective-permute-done.3 = bf16[2,128,256]{2,1,0:T(8,128)(2,1)S(1)} collective-permute-done((bf16[2,128,256]{2,1,0:T(8,128)(2,1)S(1)}, bf16[2,128,256]{2,1,0:T(8,128)(2,1)S(1)}, u32[]{:S(2)}, u32[]{:S(2)}) %collective-permute-start.3) | collective-permute-done | bytes 131104 | tf_op jit(solution)/shard_map/ppermute | solution.py:366
  38.6 0.1 maximum_add_fusion
  38.7 2.4 %collective-permute-start.4 = (bf16[2,1,128,256]{3,2,1,0:T(8,128)(2,1)S(1)}, bf16[2,1,128,256]{3,2,1,0:T(8,128)(2,1)S(1)}, u32[]{:S(2)}, u32[]{:S(2)}) collective-permute-start(bf16[2,1,128,256]{3,2,1,0:T(8,128)(2,1)S(1)} %slice.38), channel_id=1, source_target_pairs={{0,16},{4,20},{8,24},{12,28},{16,0},{20,4},{24,8},{28,12},{1,17},{... | collective-permute-start | bytes 393224 | tf_op jit(solution)/shard_map/ppermute | solution.py:366
  41.2 4.9 %collective-permute-done.4.got_ref = bf16[2,1,128,256]{3,2,1,0:T(8,128)(2,1)S(1)} collective-permute-done((bf16[2,1,128,256]{3,2,1,0:T(8,128)(2,1)S(1)}, bf16[2,1,128,256]{3,2,1,0:T(8,128)(2,1)S(1)}, u32[]{:S(2)}, u32[]{:S(2)}) %collective-permute-start.4) | collective-permute-done | bytes 131104 | tf_op jit(solution)/shard_map/ppermute | solution.py:366
  46.1 0.1 collective-permute-start.5
  46.2 1.3 %collective-permute-done.5 = f32[128,256]{1,0:T(8,128)S(1)} collective-permute-done((f32[128,256]{1,0:T(8,128)S(1)}, f32[128,256]{1,0:T(8,128)S(1)}, u32[]{:S(2)}, u32[]{:S(2)}) %collective-permute-start.5) | collective-permute-done | bytes 131104 | tf_op jit(solution)/shard_map/ppermute | solution.py:366
  47.5 1.6 %collective-permute-start.6 = (bf16[128,256]{1,0:T(8,128)(2,1)S(1)}, bf16[128,256]{1,0:T(8,128)(2,1)S(1)}, u32[]{:S(2)}, u32[]{:S(2)}) collective-permute-start(bf16[128,256]{1,0:T(8,128)(2,1)S(1)} %add_convert_fusion.mean_ref), channel_id=1, source_target_pairs={{0,2},{1,3},{2,0},{3,1},{4,6},{5,7},{6,4},{7,5},{8,10},{9,11},{10,... | collective-permute-start | bytes 196616 | tf_op jit(solution)/shard_map/ppermute | solution.py:366
  49.1 2.7 %collective-permute-done.6.got_ref = bf16[128,256]{1,0:T(8,128)(2,1)S(1)} collective-permute-done((bf16[128,256]{1,0:T(8,128)(2,1)S(1)}, bf16[128,256]{1,0:T(8,128)(2,1)S(1)}, u32[]{:S(2)}, u32[]{:S(2)}) %collective-permute-start.6) | collective-permute-done | bytes 65568 | tf_op jit(solution)/shard_map/ppermute | solution.py:366
  51.9 0.3 shard_map.133
  52.1 0.1 collective-permute-start.7
  52.2 1.2 %collective-permute-done.7.other_ref = f32[64,128]{1,0:T(8,128)S(1)} collective-permute-done((f32[64,128]{1,0:T(8,128)S(1)}, f32[64,128]{1,0:T(8,128)S(1)}, u32[]{:S(2)}, u32[]{:S(2)}) %collective-permute-start.7) | collective-permute-done | bytes 32800 | tf_op jit(solution)/shard_map/ppermute | solution.py:366
  53.4 0.2 shard_map.134
  53.6 0.5 collective-permute-start.10
  54.2 2.4 %collective-permute-start.9 = (f32[64,256]{1,0:T(8,128)S(1)}, f32[64,256]{1,0:T(8,128)S(1)}, u32[]{:S(2)}, u32[]{:S(2)}) collective-permute-start(f32[64,256]{1,0:T(8,128)S(1)} %get-tuple-element.27), channel_id=1, source_target_pairs={{0,8},{4,12},{8,0},{12,4},{16,24},{20,28},{24,16},{28,20},{1,9},{5... | collective-permute-start | bytes 196616 | tf_op jit(solution)/shard_map/ppermute | solution.py:366
  56.6 0.6 collective-permute-start.8
  57.2 2.4 %collective-permute-done.10 = f32[64,256]{1,0:T(8,128)S(1)} collective-permute-done((f32[64,256]{1,0:T(8,128)S(1)}, f32[64,256]{1,0:T(8,128)S(1)}, u32[]{:S(2)}, u32[]{:S(2)}) %collective-permute-start.10) | collective-permute-done | bytes 65568 | tf_op jit(solution)/shard_map/ppermute | solution.py:366
  59.5 0.6 collective-permute-done.9
  60.1 0.7 %collective-permute-done.8 = f32[64,256]{1,0:T(8,128)S(1)} collective-permute-done((f32[64,256]{1,0:T(8,128)S(1)}, f32[64,256]{1,0:T(8,128)S(1)}, u32[]{:S(2)}, u32[]{:S(2)}) %collective-permute-start.8) | collective-permute-done | bytes 65568 | tf_op jit(solution)/shard_map/ppermute | solution.py:366
  60.9 1.1 %collective-permute-start.11 = (f32[64,256]{1,0:T(8,128)S(1)}, f32[64,256]{1,0:T(8,128)S(1)}, u32[]{:S(2)}, u32[]{:S(2)}) collective-permute-start(f32[64,256]{1,0:T(8,128)S(1)} %add_add_fusion), channel_id=1, source_target_pairs={{0,16},{4,20},{8,24},{12,28},{16,0},{20,4},{24,8},{28,12},{1,17},{... | collective-permute-start | bytes 196616 | tf_op jit(solution)/shard_map/ppermute | solution.py:366
  62.0 4.3 %collective-permute-done.11 = f32[64,256]{1,0:T(8,128)S(1)} collective-permute-done((f32[64,256]{1,0:T(8,128)S(1)}, f32[64,256]{1,0:T(8,128)S(1)}, u32[]{:S(2)}, u32[]{:S(2)}) %collective-permute-start.11) | collective-permute-done | bytes 65568 | tf_op jit(solution)/shard_map/ppermute | solution.py:366
  66.3 0.1 collective-permute-start.12
  66.4 1.2 %collective-permute-done.12.far_ref = f32[64,256]{1,0:T(8,128)S(1)} collective-permute-done((f32[64,256]{1,0:T(8,128)S(1)}, f32[64,256]{1,0:T(8,128)S(1)}, u32[]{:S(2)}, u32[]{:S(2)}) %collective-permute-start.12) | collective-permute-done | bytes 65568 | tf_op jit(solution)/shard_map/ppermute | solution.py:366
  67.6 3.3 %shard_map.135 = (f32[64,512]{1,0:T(8,128)}, f32[128,512]{1,0:T(8,128)}, f32[128,512]{1,0:T(8,128)}) custom-call(f32[64,256]{1,0:T(8,128)S(1)} %add.31.near_ref, f32[64,256]{1,0:T(8,128)S(1)} %collective-permute-done.12.far_ref, f32[64,128]{1,0:T(8,128)S(1)} %get-tuple-element.28.left_ref, f32[128,256]{1,0:T(8,128)S(1)} %get-tuple-element.23.near_matrix_ref, ...), custom_call_target="tpu_custom_call" | custom-call | tf_op jit(solution)/shard_map/pallas_call | solution.py:530
  (13 shorter events, 0.2 us)
Async XLA Ops:
  2.6 14.6 %all-to-all-start = ((bf16[8,8,512]{2,1,0:T(8,128)(2,1)}), bf16[8,8,512]{2,1,0:T(8,128)(2,1)S(1)}, u32[]{:S(2)}, u32[]{:S(2)}) async-start(bf16[8,8,512]{2,1,0:T(8,128)(2,1)} %bitcast.27), calls=%async_computation | async-start | bytes 131072 | tf_op jit(solution)/shard_map/all_to_all | solution.py:406
  9.9 7.3 %copy-start = (bf16[1,512,512]{2,1,0:T(8,128)(2,1)S(1)}, bf16[1,512,512]{2,1,0:T(8,128)(2,1)}, u32[]{:S(2)}) copy-start(bf16[1,512,512]{2,1,0:T(8,128)(2,1)} %param.10) | copy-start | bytes 1572868
  9.9 7.3 %copy-start.1 = (bf16[1024,512]{1,0:T(8,128)(2,1)S(1)}, bf16[1024,512]{1,0:T(8,128)(2,1)}, u32[]{:S(2)}) copy-start(bf16[1024,512]{1,0:T(8,128)(2,1)} %wnode_ref.1) | copy-start | bytes 3145732
  9.9 7.3 %copy-start.2 = (bf16[1,512,512]{2,1,0:T(8,128)(2,1)S(1)}, bf16[1,512,512]{2,1,0:T(8,128)(2,1)}, u32[]{:S(2)}) copy-start(bf16[1,512,512]{2,1,0:T(8,128)(2,1)} %param.15) | copy-start | bytes 1572868
  9.9 7.3 %copy-start.5 = (s32[1,2048]{1,0:T(1,128)S(1)}, s32[1,2048]{1,0:T(1,128)}, u32[]{:S(2)}) copy-start(s32[1,2048]{1,0:T(1,128)} %send_ref.1) | copy-start | bytes 24580
  9.9 7.3 %copy-start.6 = (s32[1,2048]{1,0:T(1,128)S(1)}, s32[1,2048]{1,0:T(1,128)}, u32[]{:S(2)}) copy-start(s32[1,2048]{1,0:T(1,128)} %recv_ref.1) | copy-start | bytes 24580
  23.7 7.8 %collective-permute-start = (bf16[4,128,256]{2,1,0:T(8,128)(2,1)S(1)}, bf16[4,128,256]{2,1,0:T(8,128)(2,1)S(1)}, u32[]{:S(2)}, u32[]{:S(2)}) collective-permute-start(bf16[4,128,256]{2,1,0:T(8,128)(2,1)S(1)} %get-tuple-element.20), channel_id=1, source_target_pairs={{0,4},{4,0},{8,12},{12,8},{16,20},{20,16},{24,28},{28,24},{1,5},{5... | collective-permute-start | bytes 786440 | tf_op jit(solution)/shard_map/ppermute | solution.py:366
  25.8 7.7 %collective-permute-start.1 = (bf16[4,128,256]{2,1,0:T(8,128)(2,1)S(1)}, bf16[4,128,256]{2,1,0:T(8,128)(2,1)S(1)}, u32[]{:S(2)}, u32[]{:S(2)}) collective-permute-start(bf16[4,128,256]{2,1,0:T(8,128)(2,1)S(1)} %get-tuple-element.22), channel_id=1, source_target_pairs={{0,8},{4,12},{8,0},{12,4},{16,24},{20,28},{24,16},{28,20},{1,9},{5... | collective-permute-start | bytes 786440 | tf_op jit(solution)/shard_map/ppermute | solution.py:366
  31.7 5.0 %collective-permute-start.2 = (bf16[2,128,256]{2,1,0:T(8,128)(2,1)S(1)}, bf16[2,128,256]{2,1,0:T(8,128)(2,1)S(1)}, u32[]{:S(2)}, u32[]{:S(2)}) collective-permute-start(bf16[2,128,256]{2,1,0:T(8,128)(2,1)S(1)} %slice.40), channel_id=1, source_target_pairs={{0,8},{4,12},{8,0},{12,4},{16,24},{20,28},{24,16},{28,20},{1,9},{5... | collective-permute-start | bytes 393224 | tf_op jit(solution)/shard_map/ppermute | solution.py:366
  33.5 12.6 %copy-start.4 = (f32[1,128,512]{2,1,0:T(8,128)S(1)}, f32[1,128,512]{2,1,0:T(8,128)}, u32[]{:S(2)}) copy-start(f32[1,128,512]{2,1,0:T(8,128)} %param.18) | copy-start | bytes 786436
  33.6 18.3 %copy-start.3 = (f32[512,64]{0,1:T(8,128)S(1)}, f32[512,64]{0,1:T(8,128)}, u32[]{:S(2)}) copy-start(f32[512,64]{0,1:T(8,128)} %param.19) | copy-start | bytes 393220
  33.6 5.0 %collective-permute-start.3 = (bf16[2,128,256]{2,1,0:T(8,128)(2,1)S(1)}, bf16[2,128,256]{2,1,0:T(8,128)(2,1)S(1)}, u32[]{:S(2)}, u32[]{:S(2)}) collective-permute-start(bf16[2,128,256]{2,1,0:T(8,128)(2,1)S(1)} %slice.39), channel_id=1, source_target_pairs={{0,4},{4,0},{8,12},{12,8},{16,20},{20,16},{24,28},{28,24},{1,5},{5... | collective-permute-start | bytes 393224 | tf_op jit(solution)/shard_map/ppermute | solution.py:366
  38.7 7.3 %collective-permute-start.4 = (bf16[2,1,128,256]{3,2,1,0:T(8,128)(2,1)S(1)}, bf16[2,1,128,256]{3,2,1,0:T(8,128)(2,1)S(1)}, u32[]{:S(2)}, u32[]{:S(2)}) collective-permute-start(bf16[2,1,128,256]{3,2,1,0:T(8,128)(2,1)S(1)} %slice.38), channel_id=1, source_target_pairs={{0,16},{4,20},{8,24},{12,28},{16,0},{20,4},{24,8},{28,12},{1,17},{... | collective-permute-start | bytes 393224 | tf_op jit(solution)/shard_map/ppermute | solution.py:366
  46.1 1.4 %collective-permute-start.5 = (f32[128,256]{1,0:T(8,128)S(1)}, f32[128,256]{1,0:T(8,128)S(1)}, u32[]{:S(2)}, u32[]{:S(2)}) collective-permute-start(f32[128,256]{1,0:T(8,128)S(1)} %get-tuple-element.24.far_matrix_ref), channel_id=1, source_target_pairs={{0,1},{1,0},{2,3},{3,2},{4,5},{5,4},{6,7},{7,6},{8,9},{9,8},{10,11... | collective-permute-start | bytes 393224 | tf_op jit(solution)/shard_map/ppermute | solution.py:366
  47.5 4.3 %collective-permute-start.6 = (bf16[128,256]{1,0:T(8,128)(2,1)S(1)}, bf16[128,256]{1,0:T(8,128)(2,1)S(1)}, u32[]{:S(2)}, u32[]{:S(2)}) collective-permute-start(bf16[128,256]{1,0:T(8,128)(2,1)S(1)} %add_convert_fusion.mean_ref), channel_id=1, source_target_pairs={{0,2},{1,3},{2,0},{3,1},{4,6},{5,7},{6,4},{7,5},{8,10},{9,11},{10,... | collective-permute-start | bytes 196616 | tf_op jit(solution)/shard_map/ppermute | solution.py:366
  52.1 1.3 %collective-permute-start.7 = (f32[64,128]{1,0:T(8,128)S(1)}, f32[64,128]{1,0:T(8,128)S(1)}, u32[]{:S(2)}, u32[]{:S(2)}) collective-permute-start(f32[64,128]{1,0:T(8,128)S(1)} %get-tuple-element.25.left_ref), channel_id=1, source_target_pairs={{0,1},{1,0},{2,3},{3,2},{4,5},{5,4},{6,7},{7,6},{8,9},{9,8},{10,11... | collective-permute-start | bytes 98312 | tf_op jit(solution)/shard_map/ppermute | solution.py:366
  53.6 5.9 %collective-permute-start.10 = (f32[64,256]{1,0:T(8,128)S(1)}, f32[64,256]{1,0:T(8,128)S(1)}, u32[]{:S(2)}, u32[]{:S(2)}) collective-permute-start(f32[64,256]{1,0:T(8,128)S(1)} %get-tuple-element.27), channel_id=1, source_target_pairs={{0,12},{4,8},{8,4},{12,0},{16,28},{20,24},{24,20},{28,16},{1,13},{... | collective-permute-start | bytes 196616 | tf_op jit(solution)/shard_map/ppermute | solution.py:366
  54.2 6.0 %collective-permute-start.9 = (f32[64,256]{1,0:T(8,128)S(1)}, f32[64,256]{1,0:T(8,128)S(1)}, u32[]{:S(2)}, u32[]{:S(2)}) collective-permute-start(f32[64,256]{1,0:T(8,128)S(1)} %get-tuple-element.27), channel_id=1, source_target_pairs={{0,8},{4,12},{8,0},{12,4},{16,24},{20,28},{24,16},{28,20},{1,9},{5... | collective-permute-start | bytes 196616 | tf_op jit(solution)/shard_map/ppermute | solution.py:366
  56.6 4.3 %collective-permute-start.8 = (f32[64,256]{1,0:T(8,128)S(1)}, f32[64,256]{1,0:T(8,128)S(1)}, u32[]{:S(2)}, u32[]{:S(2)}) collective-permute-start(f32[64,256]{1,0:T(8,128)S(1)} %get-tuple-element.27), channel_id=1, source_target_pairs={{0,4},{4,0},{8,12},{12,8},{16,20},{20,16},{24,28},{28,24},{1,5},{5... | collective-permute-start | bytes 196616 | tf_op jit(solution)/shard_map/ppermute | solution.py:366
  60.9 5.4 %collective-permute-start.11 = (f32[64,256]{1,0:T(8,128)S(1)}, f32[64,256]{1,0:T(8,128)S(1)}, u32[]{:S(2)}, u32[]{:S(2)}) collective-permute-start(f32[64,256]{1,0:T(8,128)S(1)} %add_add_fusion), channel_id=1, source_target_pairs={{0,16},{4,20},{8,24},{12,28},{16,0},{20,4},{24,8},{28,12},{1,17},{... | collective-permute-start | bytes 196616 | tf_op jit(solution)/shard_map/ppermute | solution.py:366
  66.3 1.3 %collective-permute-start.12 = (f32[64,256]{1,0:T(8,128)S(1)}, f32[64,256]{1,0:T(8,128)S(1)}, u32[]{:S(2)}, u32[]{:S(2)}) collective-permute-start(f32[64,256]{1,0:T(8,128)S(1)} %add.31.near_ref), channel_id=1, source_target_pairs={{0,1},{1,0},{2,3},{3,2},{4,5},{5,4},{6,7},{7,6},{8,9},{9,8},{10,11... | collective-permute-start | bytes 196616 | tf_op jit(solution)/shard_map/ppermute | solution.py:366
